TPU v7x, 512 devices: a whole 4x8x8 slice. The times are simulated.
512 devices in a mesh: py: 16 (over x, z_lo, core), px: 32 (over y, z_hi).
Axes of the slice: x: 4, y: 8, z: 8 (z_hi: 4, z_lo: 2; z = z_hi * 2 + z_lo), core: 2. Of those that a mesh axis runs over, the one named last changes fastest.
Arguments:
- forcing: float32 [1024, 32, 1024], P('px', 'py')
- inv_density: float32 [1024, 32, 1024], P('px', 'py'), may hold values from 0.5 to 4
- stretch_x: float32 [1024], P('px'), may hold values from 0.5 to 2
- stretch_y: float32 [32], P('py'), may hold values from 0.5 to 2
- stretch_z: float32 [1024], replicated, may hold values from 0.5 to 2
- lines_z0: float32 [4, 256, 256], replicated
- lines_x0: float32 [4, 256, 256], replicated
- lines_z1: float32 [2, 256, 256], replicated
- lines_x1: float32 [2, 256, 256], replicated
- coarse_inverse: float32 [512, 512], P(('py', 'px')), as said below
Outputs:
- pressure_adjoint: float32 [1024, 32, 1024], P('px', 'py')
Inputs may be any that keep to these rules, and one draw needn't show every extreme that they name: coarse_inverse is symmetric.
All inputs are finite; a program needn't handle non-finite values.
Results may differ from a plain program's by a relative error of at most 0.0001.
Values sent between devices are 32-bit elements; how exact they have to be, the bound alone decides.
No kernel may reach another device: no remote copies, remote signals or barrier semaphores. Data moves between devices by JAX's collectives and lax.ppermute only.
A program may use at most 64 MiB of HBM per device.

v0:
```python
import jax
import jax.numpy as jnp
from jax import lax
from jax.experimental import pallas as pl
from jax.experimental.pallas import tpu as pltpu
from jax.sharding import PartitionSpec as P


shift_term = 0.1
f32 = jnp.float32
bf16 = jnp.bfloat16

N_PY, N_PX = 16, 32
FX, FZ = 32, 1024
MX, MZ = 16, 512
FH, MH = 8, 4
FE, ME = FX + 2 * FH, MX + 2 * MH


def roll(v, shift, axis):
    return pltpu.roll(v, shift % v.shape[axis], axis)


def dyn(ref, start, size):
    return ref[pl.ds(pl.multiple_of(start, 8), size), :]


def halves(a):
    high = a.astype(bf16)
    return high, (a - high.astype(f32)).astype(bf16)


def thirds(a):
    high, rest = a.astype(bf16), None
    rest = a - high.astype(f32)
    middle = rest.astype(bf16)
    return high, middle, (rest - middle.astype(f32)).astype(bf16)


def product(a, b, dims):
    return lax.dot_general(a, b, (dims, ((), ())), preferred_element_type=f32)


def dot(a, b, dims=((1,), (0,))):
    a_high, a_low = halves(a)
    b_high, b_low = halves(b)
    return product(a_high, b_high, dims) + (product(a_high, b_low, dims) + product(a_low, b_high, dims))


def pick_right(a, weight):
    dims = ((1,), (0,))
    w = weight.astype(bf16)
    high, middle, low = thirds(a)
    return product(high, w, dims) + (product(middle, w, dims) + product(low, w, dims))


def pick_left(weight, a):
    dims = ((1,), (0,))
    w = weight.astype(bf16)
    high, middle, low = thirds(a)
    return product(w, high, dims) + (product(w, middle, dims) + product(w, low, dims))


def iota(shape, axis):
    return lax.broadcasted_iota(jnp.int32, shape, axis)


def rows_of(rows):
    at = iota((8, rows[0].shape[1]), 0)
    total = jnp.zeros((8, rows[0].shape[1]), f32)
    for i, row in enumerate(rows):
        total = jnp.where(at == i, row, total)
    return total


def rows_at(pairs):
    at = iota((8, pairs[0][1].shape[1]), 0)
    total = jnp.zeros((8, pairs[0][1].shape[1]), f32)
    for i, row in pairs:
        total = jnp.where(at == i, row, total)
    return total


def near_z(v):
    lane = iota(v.shape, 1)
    last = v.shape[1] - 1
    below = jnp.where(lane == 0, 0.0, roll(v, 1, 1))
    above = jnp.where(lane == last, 0.0, roll(v, -1, 1))
    return below + above


def near_x(v):
    return roll(v, 1, 0) + roll(v, -1, 0)


def operate(v, v_near_x, v_near_y, rho, cx, cy, cz):
    twice = 2.0 * v
    stencil = cx * (twice - v_near_x) + cy * (twice - v_near_y) + cz * (twice - near_z(v))
    return shift_term * v + rho * stencil


def diagonal(rho, cx, cy, cz):
    return shift_term + 2.0 * rho * (cx + cy + cz)


def solve_z(w, lines):
    count, size = lines.shape[0], lines.shape[1]
    parts = []
    for k in range(count):
        parts.append(dot(w[:, k * size : (k + 1) * size], lines[k], ((1,), (1,))))
    return jnp.concatenate(parts, axis=1)


def columns_by(v, pick):
    cuts = [slice(256 * k, 256 * (k + 1)) for k in range(v.shape[1] // 256)]
    return jnp.concatenate([pick_right(v[:, cut], pick) for cut in cuts], axis=1)


def pair_columns(v, scale):
    fine, coarse = iota((256, 128), 0), iota((256, 128), 1)
    return columns_by(v, jnp.where(fine // 2 == coarse, scale, 0.0))


def even_columns(v, scale):
    fine, coarse = iota((256, 128), 0), iota((256, 128), 1)
    return columns_by(v, jnp.where(fine == 2 * coarse, scale, 0.0))


def restrict_columns(v):
    lane = iota(v.shape, 1)
    last = v.shape[1] - 1
    one = jnp.where(lane == last, 0.0, roll(v, -1, 1))
    two = jnp.where(lane >= last - 1, 0.0, roll(v, -2, 1))
    below = jnp.where(lane == 0, 0.0, roll(v, 1, 1))
    return even_columns(below + 3.0 * v + 3.0 * one + two, 0.125)


def raise_columns(v):
    lane = iota(v.shape, 1)
    last = v.shape[1] - 1
    below = jnp.where(lane == 0, 0.0, roll(v, 1, 1))
    above = jnp.where(lane == last, 0.0, roll(v, -1, 1))
    even = 3.0 * v + below
    odd = 3.0 * v + above
    coarse, fine = iota((128, 256), 0), iota((128, 256), 1)
    at_even = jnp.where(fine == 2 * coarse, 0.25, 0.0)
    at_odd = jnp.where(fine == 2 * coarse + 1, 0.25, 0.0)
    parts = []
    for k in range(v.shape[1] // 128):
        cut = slice(128 * k, 128 * (k + 1))
        parts.append(pick_right(even[:, cut], at_even) + pick_right(odd[:, cut], at_odd))
    return jnp.concatenate(parts, axis=1)


def restrict_rows(v):
    coarse, fine = iota((ME, FE), 0), iota((ME, FE), 1)
    away = fine - 2 * coarse
    weight = jnp.where((away == 0) | (away == 1), 0.375, 0.0)
    weight = weight + jnp.where((away == -1) | (away == 2), 0.125, 0.0)
    return pick_left(weight, v)


def pair_rows(v):
    coarse, fine = iota((ME, FE), 0), iota((ME, FE), 1)
    return pick_left(jnp.where(fine // 2 == coarse, 1.0, 0.0), v)


def raise_rows(v):
    fine, coarse = iota((FE, ME), 0), iota((FE, ME), 1)
    away = fine - 2 * coarse
    weight = jnp.where((away == 0) | (away == 1), 0.75, 0.0)
    weight = weight + jnp.where((away == 2) | (away == -1), 0.25, 0.0)
    return pick_left(weight, v)


def inside_middle(px):
    row = iota((ME, MZ), 0) + MX * px - MH
    return (row >= 0) & (row < MX * N_PX)


def inside_fine(px):
    row = iota((FE, FZ), 0) + FX * px - FH
    return (row >= 0) & (row < FX * N_PX)


def to_slabs(plane, out, at):
    for m in range(8):
        out[m, at] = plane[:, 128 * m : 128 * (m + 1)]


def from_slabs(ref, at):
    return jnp.concatenate([ref[m, at] for m in range(8)], axis=1)


def start(px, py, forcing, inv_density, sx, sy, force, rho, lower, upper, low, high, cx):
    square = iota((FX, FX), 0) == iota((FX, FX), 1)
    column = jnp.sum(jnp.where(square, sx[...], 0.0), axis=1, keepdims=True)
    cx[...] = jnp.broadcast_to(column, (FX, 128))
    wide = jnp.broadcast_to(column, (FX, FZ))
    edges = {}
    for at, out in ((0, lower), (1, upper)):
        f_plane, r_plane = forcing[:, at, :], inv_density[:, at, :]
        force[at] = f_plane
        rho[at] = r_plane
        out[0:32] = f_plane
        out[32:64] = r_plane
        out[64:72] = jnp.broadcast_to(sy[0:1, at : at + 1], (8, FZ))
        for row in (0, FX - 1):
            edges[at, row] = (f_plane[row : row + 1], r_plane[row : row + 1])
    for side, row, cut in ((low, 0, slice(0, 8)), (high, FX - 1, slice(24, 32))):
        for k in range(2):
            side[8 * k : 8 * k + 8] = rows_of([edges[0, row][k], edges[1, row][k]])
        side[16:24] = wide[cut]


def own_lines(px, py, force, rho, cx, sy, cz, lines, u):
    parts = []
    for at in range(2):
        parts.append(force[at] / diagonal(rho[at], cx[:, 0:1], sy[0:1, at : at + 1], cz[...]))
    solved = solve_z(jnp.concatenate(parts, axis=0), lines)
    u[0] = solved[0:FX]
    u[1] = solved[FX : 2 * FX]


def first_half(px, py, force, rho, cx, sy, cz, u, below, above, left, right, lines, slabs):
    cx_col = cx[:, 0:1]
    cz_row = cz[...]
    parts = []
    for side in (below, above):
        parts.append(side[0:32] / diagonal(side[32:64], cx_col, side[64:65], cz_row))
    cy_edge = jnp.where(iota((8, 1), 0) == 0, sy[0:1, 0:1], sy[0:1, 1:2])
    for side, row in ((left, 23), (right, 16)):
        parts.append(side[0:8] / diagonal(side[8:16], side[row : row + 1, 0:1], cy_edge, cz_row))
    solved = solve_z(jnp.concatenate(parts, axis=0), lines)
    planes = [solved[0:32], u[0], u[1], solved[32:64]]
    for at in range(2):
        own = u[at]
        before = rows_at([(7, solved[64 + at : 65 + at])])
        after = rows_at([(0, solved[72 + at : 73 + at])])
        beside_x = near_x(jnp.concatenate([before, own, after], axis=0))[FH : FH + FX]
        beside_y = planes[at] + planes[at + 2]
        cy = sy[0:1, at : at + 1]
        applied = operate(own, beside_x, beside_y, rho[at], cx_col, cy, cz_row)
        to_slabs((force[at] - applied) / diagonal(rho[at], cx_col, cy, cz_row), slabs, at)


def middle_statics(px, py, rho, cx, sy, cz, left, right, column, cx_mid, cyz_mid, told):
    coarse, fine = iota((MX, FX), 0), iota((MX, FX), 1)
    pairs = pick_left(jnp.where(fine // 2 == coarse, 1.0, 0.0), rho[0] + rho[1])
    own = pair_columns(pairs, 0.125)
    columns = jnp.concatenate([left[16:24, 0:128], cx[...], right[16:24, 0:128]], axis=0)
    cym = jnp.broadcast_to((sy[0:1, 0:1] + sy[0:1, 1:2]) * 0.125, (8, MZ))
    czm = pair_columns(jnp.broadcast_to(cz[...], (16, FZ)), 0.125)
    cx_mid[...] = pair_rows(columns) * 0.125
    cyz_mid[...] = jnp.concatenate([czm[0:1], cym[0:7]], axis=0)
    told[0:8, 0:MZ] = own[0:8]
    told[0:8, MZ:FZ] = own[8:16]
    told[8:16, 0:MZ] = jnp.broadcast_to(column[...], (8, MZ))
    told[8:16, MZ:FZ] = cym


def solve_x_fine(px, py, slabs, lines, out):
    block = lines[0]
    for at in range(2):
        column = jnp.concatenate([slabs[m, at] for m in range(8)], axis=0)
        solved = dot(block, column)
        for m in range(8):
            out[m, at] = solved[32 * m : 32 * (m + 1)]


def add_slabs(px, py, u, slabs, told, out):
    for at in range(2):
        out[FX * at : FX * (at + 1)] = u[at] + from_slabs(slabs, at)
    out[64:80] = told[...]


def half_residual(px, py, u, below, above, force, rho, y_below, y_above, cx, sy, cz, q, low, high):
    cx_col = cx[...][:, 0:1]
    cz_row = cz[...]
    us = [below[0:32], below[32:64], u[0:32], u[32:64], above[0:32], above[32:64]]
    fs = [y_below[0:32], force[0], force[1], y_above[0:32]]
    rs = [y_below[32:64], rho[0], rho[1], y_above[32:64]]
    cys = [y_below[64:65], sy[0:1, 0:1], sy[0:1, 1:2], y_above[64:65]]
    row = iota((FX, FZ), 0)
    total = None
    for j in range(4):
        own = us[j + 1]
        beside_x = jnp.where(row == 0, 0.0, roll(own, 1, 0)) + jnp.where(row == FX - 1, 0.0, roll(own, -1, 0))
        left_over = fs[j] - operate(own, beside_x, us[j] + us[j + 2], rs[j], cx_col, cys[j], cz_row)
        if j in (1, 2):
            left_over = 3.0 * left_over
        total = left_over if total is None else total + left_over
    total = total * 0.125
    q[...] = total
    for out, edge, step, cut in ((low, 0, 1, slice(0, 8)), (high, FX - 1, -1, slice(24, 32))):
        out[0:8] = total[cut]
        next_row = edge + step
        picked = [us[j + 1][edge : edge + 1] for j in range(4)]
        out[8:16] = rows_of(picked + [us[j + 1][next_row : next_row + 1] for j in range(4)])
        middle = u[64:68, 0:MZ] if edge == 0 else u[68:72, MZ:FZ]
        pairs = [jnp.concatenate([middle[2 * i : 2 * i + 1], middle[2 * i + 1 : 2 * i + 2]], axis=1) for i in range(2)]
        coarse = jnp.concatenate([u[72:73, 0:MZ], u[72:73, 0:MZ]], axis=1)
        out[16:24] = rows_of([rs[j][edge : edge + 1] for j in range(4)] + pairs + [coarse])


def to_middle(px, py, q, u, below, above, left, right, force, rho, y_below, y_above, x_left, x_right, cx, sy, cx_mid, cyz_mid, lines, u_ext, f_ext, r_ext, cx_ext, cy_ext, r_mid, f_mid, v_out, told):
    columns = jnp.concatenate([x_left[16:24, 0:128], cx[...], x_right[16:24, 0:128]], axis=0)
    cx_ext[...] = columns
    told[0:16] = below[64:80]
    told[16:32] = above[64:80]
    told[32:40] = jnp.broadcast_to(right[22:23], (8, FZ))
    told[40:48] = jnp.broadcast_to(left[22:23], (8, FZ))
    us = [below[32:64], u[0:32], u[32:64], above[0:32]]
    rs = [y_below[32:64], rho[0], rho[1], y_above[32:64]]
    cross = []
    for side, row in ((left, 0), (right, FX - 1)):
        inward = outward = None
        for j in range(4):
            weight = 0.375 if j in (1, 2) else 0.125
            here = weight * rs[j][row : row + 1] * side[8 + j : 9 + j]
            there = weight * side[16 + j : 17 + j] * us[j][row : row + 1]
            inward = here if inward is None else inward + here
            outward = there if outward is None else outward + there
        at = FH + row
        beyond = at - 1 if row == 0 else at + 1
        cross.append((at, inward * columns[at : at + 1, 0:1]))
        cross.append((beyond, outward * columns[beyond : beyond + 1, 0:1]))
    total = jnp.concatenate([left[0:8], q[...], right[0:8]], axis=0)
    line = iota((FE, FZ), 0)
    for at, term in cross:
        total = total + jnp.where(line == at, term, 0.0)
    none = jnp.zeros((8, FZ), f32)
    u_ext[0] = jnp.concatenate([none, below[0:32], none], axis=0)
    u_ext[5] = jnp.concatenate([none, above[32:64], none], axis=0)
    for j in range(4):
        before = rows_at([(7, left[8 + j : 9 + j]), (6, left[12 + j : 13 + j])])
        after = rows_at([(0, right[8 + j : 9 + j]), (1, right[12 + j : 13 + j])])
        u_ext[j + 1] = jnp.concatenate([before, us[j], after], axis=0)
    for at in range(2):
        for k, own, out in ((0, force, f_ext), (8, rho, r_ext)):
            before = rows_at([(7, x_left[k + at : k + at + 1])])
            after = rows_at([(0, x_right[k + at : k + at + 1])])
            out[at + 1] = jnp.concatenate([before, own[at], after], axis=0)
    for side, at in ((y_below, 0), (y_above, 3)):
        f_ext[at] = jnp.concatenate([none, side[0:32], none], axis=0)
        r_ext[at] = jnp.concatenate([none, side[32:64], none], axis=0)
    cy_rows = [jnp.broadcast_to(sy[0:1, at : at + 1], (1, FZ)) for at in range(2)]
    cy_ext[...] = rows_of([y_below[64:65], cy_rows[0], cy_rows[1], y_above[64:65]])
    dense = []
    for side, first in ((left, 4), (right, 0)):
        rows = []
        for i in range(2):
            line = side[20 + i : 21 + i]
            rows.append((first + 2 * i, line[:, 0:MZ]))
            rows.append((first + 2 * i + 1, line[:, MZ:FZ]))
        dense.append(rows_at(rows))
    dense[1:1] = [u[64:72, 0:MZ], u[64:72, MZ:FZ]]
    r_mid[...] = roll(jnp.concatenate(dense, axis=0), MH - 8, 0)[0:ME]
    rhs = restrict_columns(restrict_rows(total))
    rhs = jnp.where(inside_middle(px), rhs, 0.0)
    f_mid[...] = rhs
    diag = diagonal(*middle_parts(r_mid, cx_mid, cyz_mid))
    v_out[...] = solve_z(rhs / diag, lines)


def middle_parts(r_mid, cx_mid, cyz_mid):
    return r_mid[...], cx_mid[:, 0:1], cyz_mid[1:2], cyz_mid[0:1]


def middle_scaled(px, py, v, below, above, f_mid, r_mid, cx_mid, cyz_mid, out):
    rho, cx, cy, cz = middle_parts(r_mid, cx_mid, cyz_mid)
    own = v[...]
    applied = operate(own, near_x(own), below[...] + above[...], rho, cx, cy, cz)
    scaled = (f_mid[...] - applied) / diagonal(rho, cx, cy, cz)
    part = roll(scaled, -MH, 0)[0:MX]
    for i in range(out.shape[0]):
        out[i] = part


def rows_for_x(px, py, lines, out):
    place, row_of_four = px % 4, px // 4
    total = MX * N_PX
    parts = []
    for i in range(8):
        base = MX * (4 * i + place)
        pieces = [
            dyn(lines, jnp.maximum(base - 8, 0), 8),
            dyn(lines, base, MX),
            dyn(lines, jnp.minimum(base + MX, total - 8), 8),
        ]
        rows = roll(jnp.concatenate(pieces, axis=0), MH - 8, 0)[0:ME]
        at = iota((ME, 256), 0) + base - MH
        first = 256 * (row_of_four // 4)
        parts.append(jnp.where((at >= first) & (at < first + 256), rows, 0.0))
    full = jnp.concatenate(parts, axis=0)
    held = None
    for i in range(4):
        cut = jnp.where(row_of_four % 4 == i, full[:, 64 * i : 64 * (i + 1)], 0.0)
        held = cut if held is None else held + cut
    out[...] = held


def spread_x(px, py, gathered, rows, out):
    solved = dot(rows[...], gathered[...])
    for i in range(8):
        out[i] = solved[ME * i : ME * (i + 1)]


def gain_x(px, py, v, parts, out):
    total = v[...]
    for i in range(8):
        total = total + parts[i]
    out[...] = total


def solve_x_block(px, py, gathered, lines, v, out):
    total = MX * N_PX
    pieces = []
    starts = (
        (jnp.maximum(MX * px - 8, 0), 8),
        (MX * px, MX),
        (jnp.minimum(MX * px + MX, total - 8), 8),
    )
    for start, size in starts:
        pieces.append(dyn(lines, start, size))
    full = dot(jnp.concatenate(pieces, axis=0), gathered[...])
    part = roll(full, MH - 8, 0)[0:ME]
    row = iota((ME, MZ), 0) + MX * px - MH
    first = 256 * (px // 16)
    held = (row >= first) & (row < first + 256)
    out[...] = jnp.where(held, v[...] + part, 0.0)


def mend(px, py, v, other, out):
    row = iota((ME, MZ), 0)
    theirs = other[...]
    up = jnp.where((row >= MH + MX) & (px == 15), roll(theirs, MX, 0), 0.0)
    down = jnp.where((row < MH) & (px == 16), roll(theirs, -MX, 0), 0.0)
    out[...] = v[...] + (up + down)


def block_mean(px, py, v, f_mid, r_mid, cx_mid, cyz_mid, told, column, out):
    rho, cx, cy, cz = middle_parts(r_mid, cx_mid, cyz_mid)
    own = v[...]
    applied = operate(own, near_x(own), 0.0, rho, cx, cy, cz)
    row = iota((ME, MZ), 0)
    kept = jnp.where((row >= MH) & (row < MH + MX), f_mid[...] - applied, 0.0)

    def mean(a):
        return jnp.sum(jnp.sum(a, axis=0, keepdims=True), axis=1, keepdims=True) * (1.0 / (MX * MZ))

    sent = column[...] * mean(kept)
    inner = roll(own, -MH, 0)[0:MX]
    for at in (0, 16):
        share = mean(told[at : at + 8, 0:MZ] * inner[0:8] + told[at : at + 8, MZ:FZ] * inner[8:16])
        sent = sent + told[at + 8 : at + 9, 0:MZ] * (share * told[at + 8 : at + 9, MZ : MZ + 1])
    for at, edge, inner_row, mine in ((32, MH + MX, MH + MX - 1, px == 15), (40, MH - 1, MH, px == 16)):
        line = r_mid[edge : edge + 1] * cx_mid[edge : edge + 1, 0:1] * v[inner_row : inner_row + 1]
        sent = sent + told[at : at + 1, 0:MZ] * jnp.where(mine, mean(line), 0.0)
    lane = iota((8, MZ), 1)
    at_x, at_y = lane % N_PX, lane // N_PX
    wide = jnp.broadcast_to(sent, (8, MZ))
    rows = []
    for dy in (-1, 0, 1):
        for dx in (-1, 0, 1):
            held = (at_x + dx >= 0) & (at_x + dx < N_PX) & (at_y + dy >= 0) & (at_y + dy < N_PY)
            rows.append(jnp.where(held, roll(wide, -(dy * N_PX + dx), 1), 0.0)[0:1])
    stacked = jnp.concatenate([rows_of(rows[0:8]), rows_of(rows[8:9])], axis=0)
    unit = jnp.where(iota((16, 128), 0) == iota((16, 128), 1), 1.0, 0.0).astype(bf16)
    high, middle, low = thirds(stacked)
    dims = ((0,), (0,))
    out[...] = product(high, unit, dims) + (product(middle, unit, dims) + product(low, unit, dims))


def second_half(px, py, parts, v, below, above, f_mid, r_mid, cx_mid, cyz_mid, lines, out):
    total = jnp.sum(parts[...], axis=0, keepdims=True)
    row = iota((ME, MZ), 0)

    def raised(plane, dy):
        at = [total[0:1, 3 * (dy + 1) + dx : 3 * (dy + 1) + dx + 1] for dx in range(3)]
        return plane + jnp.where(row < MH, at[0], jnp.where(row < MH + MX, at[1], at[2]))

    own = raised(v[...], 0)
    beside = raised(below[...], -1) + raised(above[...], 1)
    rho, cx, cy, cz = middle_parts(r_mid, cx_mid, cyz_mid)
    applied = operate(own, near_x(own), beside, rho, cx, cy, cz)
    out[...] = own + solve_z((f_mid[...] - applied) / diagonal(rho, cx, cy, cz), lines)


def to_fine(px, py, v, below, above, far_below, far_above, u_ext, f_ext, r_ext, cx_ext, cy_ext, cz, lines, out, slabs):
    rows = [raise_rows(p[...]) for p in (far_below, below, v, above, far_above)]
    columns = raise_columns(jnp.concatenate(rows, axis=0)) * 0.25
    raised = [columns[FE * i : FE * (i + 1)] for i in range(5)]
    inside = inside_fine(px)
    us = []
    for j in range(6):
        at = 1 + j // 2
        other = at - 1 if j % 2 == 0 else at + 1
        held = inside
        if j < 2:
            held = inside & (py > 0)
        if j > 3:
            held = inside & (py < N_PY - 1)
        us.append(u_ext[j] + jnp.where(held, 3.0 * raised[at] + raised[other], 0.0))
    cx_col = cx_ext[:, 0:1]
    cz_row = cz[...]
    parts = []
    for j in range(4):
        own = us[j + 1]
        cy = cy_ext[j : j + 1]
        applied = operate(own, near_x(own), us[j] + us[j + 2], r_ext[j], cx_col, cy, cz_row)
        parts.append((f_ext[j] - applied) / diagonal(r_ext[j], cx_col, cy, cz_row))
    solved = solve_z(jnp.concatenate(parts, axis=0), lines)
    news = [us[j + 1] + solved[FE * j : FE * (j + 1)] for j in range(4)]
    inner = slice(FH, FH + FX)
    for at in range(2):
        full = news[at + 1]
        own = full[inner]
        out[at] = own
        beside_y = news[at][inner] + news[at + 2][inner]
        rho = r_ext[at + 1, inner]
        cy = cy_ext[at + 1 : at + 2]
        applied = operate(own, near_x(full)[inner], beside_y, rho, cx_col[inner], cy, cz_row)
        to_slabs((f_ext[at + 1, inner] - applied) / diagonal(rho, cx_col[inner], cy, cz_row), slabs, at)


def finish(px, py, u, slabs, out):
    for at in range(2):
        out[:, at, :] = u[at] + from_slabs(slabs, at)


class Device:
    def run(self, stage, shapes, *args, keep=()):
        used = len(args)
        args = args + tuple(keep)

        def kernel(*refs):
            refs = refs[:used] + refs[len(args) :]
            stage(lax.axis_index("px"), lax.axis_index("py"), *refs)

        whole = pl.BlockSpec(memory_space=pltpu.VMEM)
        outs = pl.pallas_call(
            kernel,
            out_shape=[jax.ShapeDtypeStruct(s, f32) for s in shapes],
            in_specs=[whole] * len(args),
            out_specs=[whole] * len(shapes),
            compiler_params=pltpu.CompilerParams(vmem_limit_bytes=24 * 1024 * 1024),
        )(*args)
        return outs if len(shapes) > 1 else outs[0]

    def local(self, fn, *args):
        return fn(*args)

    def block_of(self, lines):
        at = lax.axis_index("px") // 8
        return lax.dynamic_slice_in_dim(lines, at, 1, axis=0)

    def beside(self, axis, low, high, step=1):
        n = lax.axis_size(axis)
        up = [(i, i + step) for i in range(n - step)]
        down = [(j, i) for i, j in up]
        return lax.ppermute(high, axis, up), lax.ppermute(low, axis, down)

    def across(self, array):
        return lax.ppermute(array, "px", [(15, 16), (16, 15)])

    def everyone(self, rows):
        sent = rows.reshape(N_PX * N_PY, 1, 128)
        got = lax.all_to_all(sent, ("py", "px"), 0, 0, tiled=True)
        return got.reshape(N_PX * N_PY, 128)

    def solve_x(self, every, rows):
        fours = [list(range(k, k + 4)) for k in range(0, N_PX, 4)]
        eights = [list(range(k, N_PX, 4)) for k in range(4)]
        every = lax.all_to_all(every, "px", 0, 0, axis_index_groups=fours, tiled=True)
        parts = self.run(spread_x, [(8, ME, MZ)], every.reshape(4 * MX, MZ), rows)
        return lax.all_to_all(parts, "px", 0, 0, axis_index_groups=eights, tiled=True)

    def swap(self, axis, array, group):
        n = lax.axis_size(axis)
        groups = None
        if group < n:
            groups = [list(range(k, k + group)) for k in range(0, n, group)]
        return lax.all_to_all(array, axis, 0, 0, axis_index_groups=groups, tiled=True)


def cycle(d, forcing, inv_density, stretch_x, stretch_y, stretch_z, lines_z0, lines_x0, lines_z1, lines_x1, column):
    sx = d.local(lambda a: a.reshape(1, FX), stretch_x)
    sy = d.local(lambda a: a.reshape(1, 2), stretch_y)
    cz = d.local(lambda a: a.reshape(1, FZ), stretch_z)
    rows_x1 = d.local(lambda a: a.reshape(MX * N_PX, 256), lines_x1)
    slab, own, mid = (8, 2, FX, 128), (2, FX, FZ), (ME, MZ)

    force, rho, lower, upper, low, high, cx = d.run(
        start,
        [own, own, (72, FZ), (72, FZ), (24, FZ), (24, FZ), (FX, 128)],
        forcing, inv_density, sx, sy,
    )
    y_below, y_above = d.beside("py", lower, upper)
    x_left, x_right = d.beside("px", low, high)
    block = d.block_of(lines_x0)
    rows_x = d.run(rows_for_x, [(8 * ME, 64)], rows_x1)
    u = d.run(own_lines, [own], force, rho, cx, sy, cz, lines_z0)
    slabs = d.run(
        first_half, [slab],
        force, rho, cx, sy, cz, u, y_below, y_above, x_left, x_right, lines_z0,
    )
    slabs = d.swap("px", slabs, 8)
    cx_mid, cyz_mid, told = d.run(
        middle_statics,
        [(ME, 128), (8, MZ), (16, FZ)],
        rho, cx, sy, cz, x_left, x_right, column,
    )
    slabs = d.run(solve_x_fine, [slab], slabs, block)
    slabs = d.swap("px", slabs, 8)
    u = d.run(add_slabs, [(80, FZ)], u, slabs, told)
    below, above = d.beside("py", u, u)
    q, low, high = d.run(
        half_residual, [(FX, FZ), (24, FZ), (24, FZ)],
        u, below, above, force, rho, y_below, y_above, cx, sy, cz,
    )
    left, right = d.beside("px", low, high)
    u_ext, f_ext, r_ext, cx_ext, cy_ext, r_mid, f_mid, v, told = d.run(
        to_middle,
        [(6, FE, FZ), (4, FE, FZ), (4, FE, FZ), (FE, 128), (8, FZ), mid, mid, mid, (48, FZ)],
        q, u, below, above, left, right, force, rho, y_below, y_above, x_left, x_right,
        cx, sy, cx_mid, cyz_mid, lines_z1,
    )
    statics = (f_mid, r_mid, cx_mid, cyz_mid)
    keep = statics + (u_ext, f_ext, r_ext, cx_ext, cy_ext, cz)

    below, above = d.beside("py", v, v)
    every = d.run(middle_scaled, [(16, MX, MZ)], v, below, above, *statics, keep=keep)
    every = d.swap("px", every, 16)
    every = d.local(lambda a: a.reshape(256, MZ), every)
    v = d.run(solve_x_block, [mid], every, rows_x1, v, keep=keep)
    other = d.across(v)
    sent = d.run(block_mean, [(N_PX * N_PY, 128)], v, *statics, told, column, keep=keep)
    parts = d.everyone(sent)
    v = d.run(mend, [mid], v, other, keep=keep)
    below, above = d.beside("py", v, v)
    v = d.run(second_half, [mid], parts, v, below, above, *statics, lines_z1, keep=keep)
    below, above = d.beside("py", v, v)
    parts = d.solve_x(d.run(middle_scaled, [(4, MX, MZ)], v, below, above, *statics, keep=keep), rows_x)
    v = d.run(gain_x, [mid], v, parts, keep=keep)

    below, above = d.beside("py", v, v)
    far_below, far_above = d.beside("py", v, v, 2)
    u, slabs = d.run(
        to_fine,
        [own, slab],
        v, below, above, far_below, far_above, u_ext, f_ext, r_ext, cx_ext, cy_ext, cz, lines_z0,
    )
    slabs = d.swap("px", slabs, 8)
    slabs = d.run(solve_x_fine, [slab], slabs, block)
    slabs = d.swap("px", slabs, 8)
    return d.run(finish, [(FX, 2, FZ)], u, slabs)


def solution(mesh):
    placed = (
        P("px", "py", None),
        P("px", "py", None),
        P("px"),
        P("py"),
        P(),
        P(),
        P(),
        P(),
        P(),
        P(("py", "px"), None),
    )

    def step(*args):
        return cycle(Device(), *args)

    return jax.shard_map(
        step, mesh=mesh, in_specs=placed, out_specs=P("px", "py", None), check_vma=False
    )
```

profile of v0, /device:TPU:8, one launch (start us, length us, event | category | flops | bytes accessed | tf_op | source)
XLA Modules:
  0.0 254.3 jit_solution(15444132384471117890)
XLA Ops:
  3.5 1.8 collective-permute-start
  5.2 1.3 collective-permute-start.1
  6.5 6.1 %collective-permute-start.2 = (f32[24,1024]{1,0:T(8,128)S(1)}, f32[24,1024]{1,0:T(8,128)S(1)}, u32[]{:S(2)}, u32[]{:S(2)}) collective-permute-start(f32[24,1024]{1,0:T(8,128)S(1)} %get-tuple-element.34), channel_id=1, source_target_pairs={{0,1},{1,2},{2,3},{3,4},{4,5},{5,6},{6,7},{7,8},{8,9},{9,10},{10,1... | collective-permute-start | bytes 294920 | tf_op jit(solution)/shard_map/ppermute | solution.py:562
  12.6 6.7 %collective-permute-start.3 = (f32[24,1024]{1,0:T(8,128)S(1)}, f32[24,1024]{1,0:T(8,128)S(1)}, u32[]{:S(2)}, u32[]{:S(2)}) collective-permute-start(f32[24,1024]{1,0:T(8,128)S(1)} %get-tuple-element.35), channel_id=1, source_target_pairs={{1,0},{2,1},{3,2},{4,3},{5,4},{6,5},{7,6},{8,7},{9,8},{10,9},{11,1... | collective-permute-start | bytes 294920 | tf_op jit(solution)/shard_map/ppermute | solution.py:562
  22.5 1.5 shard_map.102
  24.0 7.6 %all-to-all-start = ((f32[8,2,32,128]{3,2,1,0:T(8,128)}), f32[8,2,32,128]{3,2,1,0:T(8,128)S(1)}, u32[]{:S(2)}, u32[]{:S(2)}) async-start(f32[8,2,32,128]{3,2,1,0:T(8,128)} %shard_map.102), calls=%async_computation | async-start | bytes 524288 | tf_op jit(solution)/shard_map/all_to_all | solution.py:584
  31.7 11.2 %all-to-all-done.refs_0_ = f32[8,2,32,128]{3,2,1,0:T(8,128)S(1)} async-done(((f32[8,2,32,128]{3,2,1,0:T(8,128)}), f32[8,2,32,128]{3,2,1,0:T(8,128)S(1)}, u32[]{:S(2)}, u32[]{:S(2)}) %all-to-all-start) | async-done | bytes 262176 | tf_op jit(solution)/shard_map/all_to_all | solution.py:584
  43.9 4.7 %all-to-all-start.1 = ((f32[8,2,32,128]{3,2,1,0:T(8,128)}), f32[8,2,32,128]{3,2,1,0:T(8,128)S(1)}, u32[]{:S(2)}, u32[]{:S(2)}) async-start(f32[8,2,32,128]{3,2,1,0:T(8,128)} %shard_map.103), calls=%async_computation.1 | async-start | bytes 524288 | tf_op jit(solution)/shard_map/all_to_all | solution.py:584
  49.2 10.2 %all-to-all-done.1.refs_1_ = f32[8,2,32,128]{3,2,1,0:T(8,128)S(1)} async-done(((f32[8,2,32,128]{3,2,1,0:T(8,128)}), f32[8,2,32,128]{3,2,1,0:T(8,128)S(1)}, u32[]{:S(2)}, u32[]{:S(2)}) %all-to-all-start.1) | async-done | bytes 262176 | tf_op jit(solution)/shard_map/all_to_all | solution.py:584
  59.4 1.4 collective-permute-start.4
  62.2 4.3 %collective-permute-done.5.refs_2_.refs_3_ = f32[80,1024]{1,0:T(8,128)S(1)} collective-permute-done((f32[80,1024]{1,0:T(8,128)S(1)}, f32[80,1024]{1,0:T(8,128)S(1)}, u32[]{:S(2)}, u32[]{:S(2)}) %collective-permute-start.5) | collective-permute-done | bytes 327712 | tf_op jit(solution)/shard_map/ppermute | solution.py:562
  67.1 2.1 collective-permute-start.6
  69.2 6.7 %collective-permute-start.7 = (f32[24,1024]{1,0:T(8,128)S(1)}, f32[24,1024]{1,0:T(8,128)S(1)}, u32[]{:S(2)}, u32[]{:S(2)}) collective-permute-start(f32[24,1024]{1,0:T(8,128)S(1)} %get-tuple-element.39), channel_id=1, source_target_pairs={{1,0},{2,1},{3,2},{4,3},{5,4},{6,5},{7,6},{8,7},{9,8},{10,9},{11,1... | collective-permute-start | bytes 294920 | tf_op jit(solution)/shard_map/ppermute | solution.py:562
  76.6 1.5 collective-permute-done.7.refs_5_
  82.1 8.4 %collective-permute-start.8 = (f32[24,512]{1,0:T(8,128)S(1)}, f32[24,512]{1,0:T(8,128)S(1)}, u32[]{:S(2)}, u32[]{:S(2)}) collective-permute-start(f32[24,512]{1,0:T(8,128)S(1)} %get-tuple-element.42.refs_0_.refs_2_), channel_id=1, source_target_pairs={{0,32},{32,64},{64,96},{96,128},{128,160},{160,192},{192,224},{224... | collective-permute-start | bytes 147464 | tf_op jit(solution)/shard_map/ppermute | solution.py:562
  91.8 1.8 collective-permute-done.9.refs_2_
  93.8 27.6 %all_to_all.40 = f32[16,16,512]{2,1,0:T(8,128)S(1)} all-to-all(f32[16,16,512]{2,1,0:T(8,128)S(1)} %shard_map.108), channel_id=1, replica_groups={{0,1,2,3,4,5,6,7,8,9,10,11,12,13,14,15},{16,17,18,19,20,21,22,23,24,25,..., dimensions={0} | all-to-all | bytes 1048576 | tf_op jit(solution)/shard_map/all_to_all | solution.py:584
  122.9 14.7 %all-to-all-start.3 = ((f32[512,1,128]{2,1,0:T(1,128)}), f32[512,1,128]{2,1,0:T(1,128)S(1)}, u32[]{:S(2)}, u32[]{:S(2)}) async-start(f32[512,1,128]{2,1,0:T(1,128)} %bitcast.14), calls=%async_computation.3 | async-start | bytes 524288 | tf_op jit(solution)/shard_map/all_to_all | solution.py:569
  139.5 2.0 collective-permute-start.11
  144.0 2.0 collective-permute-done.12.refs_3_
  146.7 7.7 %all-to-all-done.3 = f32[512,1,128]{2,1,0:T(1,128)S(1)} async-done(((f32[512,1,128]{2,1,0:T(1,128)}), f32[512,1,128]{2,1,0:T(1,128)S(1)}, u32[]{:S(2)}, u32[]{:S(2)}) %all-to-all-start.3) | async-done | bytes 262176 | tf_op jit(solution)/shard_map/all_to_all | solution.py:569
  162.1 3.2 %collective-permute-done.14.refs_2_ = f32[24,512]{1,0:T(8,128)S(1)} collective-permute-done((f32[24,512]{1,0:T(8,128)S(1)}, f32[24,512]{1,0:T(8,128)S(1)}, u32[]{:S(2)}, u32[]{:S(2)}) %collective-permute-start.14) | collective-permute-done | bytes 49184 | tf_op jit(solution)/shard_map/ppermute | solution.py:562
  166.0 3.3 %all-to-all-start.4 = ((f32[4,16,512]{2,1,0:T(8,128)}), f32[4,16,512]{2,1,0:T(8,128)S(1)}, u32[]{:S(2)}, u32[]{:S(2)}) async-start(f32[4,16,512]{2,1,0:T(8,128)} %shard_map.113), calls=%async_computation.4 | async-start | bytes 262144 | tf_op jit(solution)/shard_map/all_to_all | solution.py:575
  170.6 7.4 %all-to-all-done.4 = f32[4,16,512]{2,1,0:T(8,128)S(1)} async-done(((f32[4,16,512]{2,1,0:T(8,128)}), f32[4,16,512]{2,1,0:T(8,128)S(1)}, u32[]{:S(2)}, u32[]{:S(2)}) %all-to-all-start.4) | async-done | bytes 131104 | tf_op jit(solution)/shard_map/all_to_all | solution.py:575
  178.3 26.9 %all_to_all.41.refs_1_ = f32[8,24,512]{2,1,0:T(8,128)S(1)} all-to-all(f32[8,24,512]{2,1,0:T(8,128)S(1)} %shard_map.115), channel_id=1, replica_groups={{0,4,8,12,16,20,24,28},{1,5,9,13,17,21,25,29},{2,6,10,14,18,22,26,30},{..., dimensions={0} | all-to-all | bytes 786432 | tf_op jit(solution)/shard_map/all_to_all | solution.py:577
  205.2 2.7 %collective-permute-start.15 = (f32[24,512]{1,0:T(8,128)S(1)}, f32[24,512]{1,0:T(8,128)S(1)}, u32[]{:S(2)}, u32[]{:S(2)}) collective-permute-start(f32[24,512]{1,0:T(8,128)S(1)} %shard_map.116.refs_0_), channel_id=1, source_target_pairs={{0,32},{32,64},{64,96},{96,128},{128,160},{160,192},{192,224},{224... | collective-permute-start | bytes 147464 | tf_op jit(solution)/shard_map/ppermute | solution.py:562
  209.2 7.5 %collective-permute-start.17 = (f32[24,512]{1,0:T(8,128)S(1)}, f32[24,512]{1,0:T(8,128)S(1)}, u32[]{:S(2)}, u32[]{:S(2)}) collective-permute-start(f32[24,512]{1,0:T(8,128)S(1)} %shard_map.116.refs_0_), channel_id=1, source_target_pairs={{0,64},{32,96},{64,128},{96,160},{128,192},{160,224},{192,256},{22... | collective-permute-start | bytes 147464 | tf_op jit(solution)/shard_map/ppermute | solution.py:562
  216.7 1.5 collective-permute-start.18
  218.5 4.3 %collective-permute-done.18.refs_4_ = f32[24,512]{1,0:T(8,128)S(1)} collective-permute-done((f32[24,512]{1,0:T(8,128)S(1)}, f32[24,512]{1,0:T(8,128)S(1)}, u32[]{:S(2)}, u32[]{:S(2)}) %collective-permute-start.18) | collective-permute-done | bytes 49184 | tf_op jit(solution)/shard_map/ppermute | solution.py:562
  222.7 2.7 %shard_map.117 = (f32[2,32,1024]{2,1,0:T(8,128)S(1)}, f32[8,2,32,128]{3,2,1,0:T(8,128)S(1)}) custom-call(f32[24,512]{1,0:T(8,128)S(1)} %shard_map.116.refs_0_, f32[24,512]{1,0:T(8,128)S(1)} %collective-permute-done.15.refs_1_, f32[24,512]{1,0:T(8,128)S(1)} %collective-permute-done.16.refs_2_, f32[24,512]{1,0:T(8,128)S(1)} %collective-permute-done.17.refs_3_, ...), custom_call_target="tpu_custom_call" | custom-call | tf_op jit(solution)/shard_map/pallas_call | solution.py:542
  225.4 13.6 %all_to_all.42.refs_0_ = f32[8,2,32,128]{3,2,1,0:T(8,128)S(1)} all-to-all(f32[8,2,32,128]{3,2,1,0:T(8,128)S(1)} %get-tuple-element.52), channel_id=1, replica_groups={{0,1,2,3,4,5,6,7},{8,9,10,11,12,13,14,15},{16,17,18,19,20,21,22,23},{24..., dimensions={0} | all-to-all | bytes 524288 | tf_op jit(solution)/shard_map/all_to_all | solution.py:584
  239.4 14.2 %all_to_all.43.refs_1_ = f32[8,2,32,128]{3,2,1,0:T(8,128)S(1)} all-to-all(f32[8,2,32,128]{3,2,1,0:T(8,128)S(1)} %shard_map.118), channel_id=1, replica_groups={{0,1,2,3,4,5,6,7},{8,9,10,11,12,13,14,15},{16,17,18,19,20,21,22,23},{24..., dimensions={0} | all-to-all | bytes 524288 | tf_op jit(solution)/shard_map/all_to_all | solution.py:584
  (115 shorter events, 35.2 us)
Async XLA Ops:
  0.0 31.6 %copy-start = (f32[4,256,256]{2,1,0:T(8,128)S(1)}, f32[4,256,256]{2,1,0:T(8,128)}, u32[]{:S(2)}) copy-start(f32[4,256,256]{2,1,0:T(8,128)} %param.16) | copy-start | bytes 3145732
  3.4 63.1 %copy-start.7 = (f32[2,32,1024]{2,1,0:T(8,128)}, f32[2,32,1024]{2,1,0:T(8,128)S(1)}, u32[]{:S(2)}) copy-start(f32[2,32,1024]{2,1,0:T(8,128)S(1)} %get-tuple-element.29.refs_0_.refs_3_.refs_6_) | copy-start | bytes 786436
  3.5 19.1 %collective-permute-start = (f32[72,1024]{1,0:T(8,128)S(1)}, f32[72,1024]{1,0:T(8,128)S(1)}, u32[]{:S(2)}, u32[]{:S(2)}) collective-permute-start(f32[72,1024]{1,0:T(8,128)S(1)} %get-tuple-element.32), channel_id=1, source_target_pairs={{0,32},{32,64},{64,96},{96,128},{128,160},{160,192},{192,224},{224... | collective-permute-start | bytes 884744 | tf_op jit(solution)/shard_map/ppermute | solution.py:562
  5.2 17.3 %collective-permute-start.1 = (f32[72,1024]{1,0:T(8,128)S(1)}, f32[72,1024]{1,0:T(8,128)S(1)}, u32[]{:S(2)}, u32[]{:S(2)}) collective-permute-start(f32[72,1024]{1,0:T(8,128)S(1)} %get-tuple-element.33), channel_id=1, source_target_pairs={{32,0},{64,32},{96,64},{128,96},{160,128},{192,160},{224,192},{256... | collective-permute-start | bytes 884744 | tf_op jit(solution)/shard_map/ppermute | solution.py:562
  6.5 15.3 %collective-permute-start.2 = (f32[24,1024]{1,0:T(8,128)S(1)}, f32[24,1024]{1,0:T(8,128)S(1)}, u32[]{:S(2)}, u32[]{:S(2)}) collective-permute-start(f32[24,1024]{1,0:T(8,128)S(1)} %get-tuple-element.34), channel_id=1, source_target_pairs={{0,1},{1,2},{2,3},{3,4},{4,5},{5,6},{6,7},{7,8},{8,9},{9,10},{10,1... | collective-permute-start | bytes 294920 | tf_op jit(solution)/shard_map/ppermute | solution.py:562
  12.6 9.9 %collective-permute-start.3 = (f32[24,1024]{1,0:T(8,128)S(1)}, f32[24,1024]{1,0:T(8,128)S(1)}, u32[]{:S(2)}, u32[]{:S(2)}) collective-permute-start(f32[24,1024]{1,0:T(8,128)S(1)} %get-tuple-element.35), channel_id=1, source_target_pairs={{1,0},{2,1},{3,2},{4,3},{5,4},{6,5},{7,6},{8,7},{9,8},{10,9},{11,1... | collective-permute-start | bytes 294920 | tf_op jit(solution)/shard_map/ppermute | solution.py:562
  22.5 44.0 %copy-start.9 = (f32[72,1024]{1,0:T(8,128)}, f32[72,1024]{1,0:T(8,128)S(1)}, u32[]{:S(2)}) copy-start(f32[72,1024]{1,0:T(8,128)S(1)} %collective-permute-done.refs_6_.refs_5_.refs_8_) | copy-start | bytes 884740
  22.5 44.0 %copy-start.11 = (f32[72,1024]{1,0:T(8,128)}, f32[72,1024]{1,0:T(8,128)S(1)}, u32[]{:S(2)}) copy-start(f32[72,1024]{1,0:T(8,128)S(1)} %collective-permute-done.1.refs_7_.refs_6_.refs_9_) | copy-start | bytes 884740
  24.0 18.8 %all-to-all-start = ((f32[8,2,32,128]{3,2,1,0:T(8,128)}), f32[8,2,32,128]{3,2,1,0:T(8,128)S(1)}, u32[]{:S(2)}, u32[]{:S(2)}) async-start(f32[8,2,32,128]{3,2,1,0:T(8,128)} %shard_map.102), calls=%async_computation | async-start | bytes 524288 | tf_op jit(solution)/shard_map/all_to_all | solution.py:584
  31.7 27.7 %copy-start.13 = (f32[1,256,256]{2,1,0:T(8,128)}, f32[1,256,256]{2,1,0:T(8,128)S(1)}, u32[]{:S(2)}) copy-start(f32[1,256,256]{2,1,0:T(8,128)S(1)} %constant_dynamic-slice_fusion.refs_1_) | copy-start | bytes 786436
  43.9 15.4 %all-to-all-start.1 = ((f32[8,2,32,128]{3,2,1,0:T(8,128)}), f32[8,2,32,128]{3,2,1,0:T(8,128)S(1)}, u32[]{:S(2)}, u32[]{:S(2)}) async-start(f32[8,2,32,128]{3,2,1,0:T(8,128)} %shard_map.103), calls=%async_computation.1 | async-start | bytes 524288 | tf_op jit(solution)/shard_map/all_to_all | solution.py:584
  59.4 2.8 %collective-permute-start.4 = (f32[80,1024]{1,0:T(8,128)S(1)}, f32[80,1024]{1,0:T(8,128)S(1)}, u32[]{:S(2)}, u32[]{:S(2)}) collective-permute-start(f32[80,1024]{1,0:T(8,128)S(1)} %shard_map.105.refs_0_.refs_1_), channel_id=1, source_target_pairs={{0,32},{32,64},{64,96},{96,128},{128,160},{160,192},{192,224},{224... | collective-permute-start | bytes 983048 | tf_op jit(solution)/shard_map/ppermute | solution.py:562
  60.9 5.6 %collective-permute-start.5 = (f32[80,1024]{1,0:T(8,128)S(1)}, f32[80,1024]{1,0:T(8,128)S(1)}, u32[]{:S(2)}, u32[]{:S(2)}) collective-permute-start(f32[80,1024]{1,0:T(8,128)S(1)} %shard_map.105.refs_0_.refs_1_), channel_id=1, source_target_pairs={{32,0},{64,32},{96,64},{128,96},{160,128},{192,160},{224,192},{256... | collective-permute-start | bytes 983048 | tf_op jit(solution)/shard_map/ppermute | solution.py:562
  67.1 9.5 %collective-permute-start.6 = (f32[24,1024]{1,0:T(8,128)S(1)}, f32[24,1024]{1,0:T(8,128)S(1)}, u32[]{:S(2)}, u32[]{:S(2)}) collective-permute-start(f32[24,1024]{1,0:T(8,128)S(1)} %get-tuple-element.38), channel_id=1, source_target_pairs={{0,1},{1,2},{2,3},{3,4},{4,5},{5,6},{6,7},{7,8},{8,9},{9,10},{10,1... | collective-permute-start | bytes 294920 | tf_op jit(solution)/shard_map/ppermute | solution.py:562
  69.2 8.9 %collective-permute-start.7 = (f32[24,1024]{1,0:T(8,128)S(1)}, f32[24,1024]{1,0:T(8,128)S(1)}, u32[]{:S(2)}, u32[]{:S(2)}) collective-permute-start(f32[24,1024]{1,0:T(8,128)S(1)} %get-tuple-element.39), channel_id=1, source_target_pairs={{1,0},{2,1},{3,2},{4,3},{5,4},{6,5},{7,6},{8,7},{9,8},{10,9},{11,1... | collective-permute-start | bytes 294920 | tf_op jit(solution)/shard_map/ppermute | solution.py:562
  82.1 39.5 %copy-start.1 = (f32[4,48,1024]{2,1,0:T(8,128)}, f32[4,48,1024]{2,1,0:T(8,128)S(1)}, u32[]{:S(2)}) copy-start(f32[4,48,1024]{2,1,0:T(8,128)S(1)} %get-tuple-element.47.refs_13_.refs_9_.refs_8_.refs_15_.refs_7_) | copy-start | bytes 2359300
  82.1 9.7 %collective-permute-start.8 = (f32[24,512]{1,0:T(8,128)S(1)}, f32[24,512]{1,0:T(8,128)S(1)}, u32[]{:S(2)}, u32[]{:S(2)}) collective-permute-start(f32[24,512]{1,0:T(8,128)S(1)} %get-tuple-element.42.refs_0_.refs_2_), channel_id=1, source_target_pairs={{0,32},{32,64},{64,96},{96,128},{128,160},{160,192},{192,224},{224... | collective-permute-start | bytes 147464 | tf_op jit(solution)/shard_map/ppermute | solution.py:562
  90.5 3.1 %collective-permute-start.9 = (f32[24,512]{1,0:T(8,128)S(1)}, f32[24,512]{1,0:T(8,128)S(1)}, u32[]{:S(2)}, u32[]{:S(2)}) collective-permute-start(f32[24,512]{1,0:T(8,128)S(1)} %get-tuple-element.42.refs_0_.refs_2_), channel_id=1, source_target_pairs={{32,0},{64,32},{96,64},{128,96},{160,128},{192,160},{224,192},{256... | collective-permute-start | bytes 147464 | tf_op jit(solution)/shard_map/ppermute | solution.py:562
  93.8 27.6 %copy-start.17 = (f32[2,256,256]{2,1,0:T(8,128)S(1)}, f32[2,256,256]{2,1,0:T(8,128)}, u32[]{:S(2)}) copy-start(f32[2,256,256]{2,1,0:T(8,128)} %param.18) | copy-start | bytes 1572868
  122.9 31.5 %all-to-all-start.3 = ((f32[512,1,128]{2,1,0:T(1,128)}), f32[512,1,128]{2,1,0:T(1,128)S(1)}, u32[]{:S(2)}, u32[]{:S(2)}) async-start(f32[512,1,128]{2,1,0:T(1,128)} %bitcast.14), calls=%async_computation.3 | async-start | bytes 524288 | tf_op jit(solution)/shard_map/all_to_all | solution.py:569
  137.6 0.7 collective-permute-start.10
  139.5 3.9 %collective-permute-start.11 = (f32[24,512]{1,0:T(8,128)S(1)}, f32[24,512]{1,0:T(8,128)S(1)}, u32[]{:S(2)}, u32[]{:S(2)}) collective-permute-start(f32[24,512]{1,0:T(8,128)S(1)} %shard_map.111.refs_1_), channel_id=1, source_target_pairs={{0,32},{32,64},{64,96},{96,128},{128,160},{160,192},{192,224},{224... | collective-permute-start | bytes 147464 | tf_op jit(solution)/shard_map/ppermute | solution.py:562
  141.5 4.5 %collective-permute-start.12 = (f32[24,512]{1,0:T(8,128)S(1)}, f32[24,512]{1,0:T(8,128)S(1)}, u32[]{:S(2)}, u32[]{:S(2)}) collective-permute-start(f32[24,512]{1,0:T(8,128)S(1)} %shard_map.111.refs_1_), channel_id=1, source_target_pairs={{32,0},{64,32},{96,64},{128,96},{160,128},{192,160},{224,192},{256... | collective-permute-start | bytes 147464 | tf_op jit(solution)/shard_map/ppermute | solution.py:562
  159.5 2.6 %collective-permute-start.13 = (f32[24,512]{1,0:T(8,128)S(1)}, f32[24,512]{1,0:T(8,128)S(1)}, u32[]{:S(2)}, u32[]{:S(2)}) collective-permute-start(f32[24,512]{1,0:T(8,128)S(1)} %shard_map.112.refs_0_), channel_id=1, source_target_pairs={{0,32},{32,64},{64,96},{96,128},{128,160},{160,192},{192,224},{224... | collective-permute-start | bytes 147464 | tf_op jit(solution)/shard_map/ppermute | solution.py:562
  160.8 4.5 %collective-permute-start.14 = (f32[24,512]{1,0:T(8,128)S(1)}, f32[24,512]{1,0:T(8,128)S(1)}, u32[]{:S(2)}, u32[]{:S(2)}) collective-permute-start(f32[24,512]{1,0:T(8,128)S(1)} %shard_map.112.refs_0_), channel_id=1, source_target_pairs={{32,0},{64,32},{96,64},{128,96},{160,128},{192,160},{224,192},{256... | collective-permute-start | bytes 147464 | tf_op jit(solution)/shard_map/ppermute | solution.py:562
  166.0 12.0 %all-to-all-start.4 = ((f32[4,16,512]{2,1,0:T(8,128)}), f32[4,16,512]{2,1,0:T(8,128)S(1)}, u32[]{:S(2)}, u32[]{:S(2)}) async-start(f32[4,16,512]{2,1,0:T(8,128)} %shard_map.113), calls=%async_computation.4 | async-start | bytes 262144 | tf_op jit(solution)/shard_map/all_to_all | solution.py:575
  178.0 27.2 %copy-start.4 = (f32[4,48,1024]{2,1,0:T(8,128)S(1)}, f32[4,48,1024]{2,1,0:T(8,128)}, u32[]{:S(2)}) copy-start(f32[4,48,1024]{2,1,0:T(8,128)} %copy-done.1) | copy-start | bytes 2359300
  205.2 33.8 %copy-start.14 = (f32[1,256,256]{2,1,0:T(8,128)S(1)}, f32[1,256,256]{2,1,0:T(8,128)}, u32[]{:S(2)}) copy-start(f32[1,256,256]{2,1,0:T(8,128)} %copy-done.13) | copy-start | bytes 786436
  205.2 13.0 %collective-permute-start.15 = (f32[24,512]{1,0:T(8,128)S(1)}, f32[24,512]{1,0:T(8,128)S(1)}, u32[]{:S(2)}, u32[]{:S(2)}) collective-permute-start(f32[24,512]{1,0:T(8,128)S(1)} %shard_map.116.refs_0_), channel_id=1, source_target_pairs={{0,32},{32,64},{64,96},{96,128},{128,160},{160,192},{192,224},{224... | collective-permute-start | bytes 147464 | tf_op jit(solution)/shard_map/ppermute | solution.py:562
  207.9 10.3 %collective-permute-start.16 = (f32[24,512]{1,0:T(8,128)S(1)}, f32[24,512]{1,0:T(8,128)S(1)}, u32[]{:S(2)}, u32[]{:S(2)}) collective-permute-start(f32[24,512]{1,0:T(8,128)S(1)} %shard_map.116.refs_0_), channel_id=1, source_target_pairs={{32,0},{64,32},{96,64},{128,96},{160,128},{192,160},{224,192},{256... | collective-permute-start | bytes 147464 | tf_op jit(solution)/shard_map/ppermute | solution.py:562
  209.2 9.3 %collective-permute-start.17 = (f32[24,512]{1,0:T(8,128)S(1)}, f32[24,512]{1,0:T(8,128)S(1)}, u32[]{:S(2)}, u32[]{:S(2)}) collective-permute-start(f32[24,512]{1,0:T(8,128)S(1)} %shard_map.116.refs_0_), channel_id=1, source_target_pairs={{0,64},{32,96},{64,128},{96,160},{128,192},{160,224},{192,256},{22... | collective-permute-start | bytes 147464 | tf_op jit(solution)/shard_map/ppermute | solution.py:562
  216.7 6.0 %collective-permute-start.18 = (f32[24,512]{1,0:T(8,128)S(1)}, f32[24,512]{1,0:T(8,128)S(1)}, u32[]{:S(2)}, u32[]{:S(2)}) collective-permute-start(f32[24,512]{1,0:T(8,128)S(1)} %shard_map.116.refs_0_), channel_id=1, source_target_pairs={{64,0},{96,32},{128,64},{160,96},{192,128},{224,160},{256,192},{28... | collective-permute-start | bytes 147464 | tf_op jit(solution)/shard_map/ppermute | solution.py:562
  (29 other events, 218.0 us)
where the time goes:
time: 256 us; the launch traced here: 254 us
  starting transfers between devices  86.9 us (34%)
  blocking collectives  82.2 us (32%)
  waiting for transfers between devices  55.2 us (22%)
  local copies, waits for them, and re-layouts  17.4 us (7%)
  Pallas kernels  12.1 us (5%)
    ppermute x18, starting transfers between devices, beside(): return (lax.ppermute(high, axis, up), lax.ppermute(low, axis, down))  55.9 us
    all_to_all x3, blocking collectives, swap(): lax.all_to_all(array, axis, 0, 0, axis_index_groups=groups, tiled=True)  55.3 us
    all_to_all x1, blocking collectives, solve_x(): lax.all_to_all(parts, 'px', 0, 0, axis_index_groups=eights, tiled=True)  26.9 us
    all_to_all x2, waiting for transfers between devices, swap(): lax.all_to_all(array, axis, 0, 0, axis_index_groups=groups, tiled=True)  21.4 us
    ppermute x18, waiting for transfers between devices, beside(): return (lax.ppermute(high, axis, up), lax.ppermute(low, axis, down))  18.6 us
    unnamed x76, local copies, waits for them, and re-layouts  17.4 us
    all_to_all x1, starting transfers between devices, everyone(): got = lax.all_to_all(sent, ('py', 'px'), 0, 0, tiled=True)  14.7 us
    all_to_all x2, starting transfers between devices, swap(): lax.all_to_all(array, axis, 0, 0, axis_index_groups=groups, tiled=True)  12.3 us
  transfers between devices with their start and end apart: 23, of which 13 were waited for; matrix products, arithmetic and copies ran while one was open for 0% of the time, Pallas kernels for 1%

commit v1 on v0

--- a/solution.py
+++ b/solution.py
@@ -530,12 +530,8 @@
 
 
 class Device:
-    def run(self, stage, shapes, *args, keep=()):
-        used = len(args)
-        args = args + tuple(keep)
-
+    def run(self, stage, shapes, *args, grant=24):
         def kernel(*refs):
-            refs = refs[:used] + refs[len(args) :]
             stage(lax.axis_index("px"), lax.axis_index("py"), *refs)
 
         whole = pl.BlockSpec(memory_space=pltpu.VMEM)
@@ -544,7 +540,7 @@
             out_shape=[jax.ShapeDtypeStruct(s, f32) for s in shapes],
             in_specs=[whole] * len(args),
             out_specs=[whole] * len(shapes),
-            compiler_params=pltpu.CompilerParams(vmem_limit_bytes=24 * 1024 * 1024),
+            compiler_params=pltpu.CompilerParams(vmem_limit_bytes=grant * 1024 * 1024),
         )(*args)
         return outs if len(shapes) > 1 else outs[0]
 
@@ -627,22 +623,21 @@
         cx, sy, cx_mid, cyz_mid, lines_z1,
     )
     statics = (f_mid, r_mid, cx_mid, cyz_mid)
-    keep = statics + (u_ext, f_ext, r_ext, cx_ext, cy_ext, cz)
 
     below, above = d.beside("py", v, v)
-    every = d.run(middle_scaled, [(16, MX, MZ)], v, below, above, *statics, keep=keep)
+    every = d.run(middle_scaled, [(16, MX, MZ)], v, below, above, *statics)
     every = d.swap("px", every, 16)
     every = d.local(lambda a: a.reshape(256, MZ), every)
-    v = d.run(solve_x_block, [mid], every, rows_x1, v, keep=keep)
+    v = d.run(solve_x_block, [mid], every, rows_x1, v)
     other = d.across(v)
-    sent = d.run(block_mean, [(N_PX * N_PY, 128)], v, *statics, told, column, keep=keep)
+    sent = d.run(block_mean, [(N_PX * N_PY, 128)], v, *statics, told, column)
     parts = d.everyone(sent)
-    v = d.run(mend, [mid], v, other, keep=keep)
+    v = d.run(mend, [mid], v, other)
     below, above = d.beside("py", v, v)
-    v = d.run(second_half, [mid], parts, v, below, above, *statics, lines_z1, keep=keep)
+    v = d.run(second_half, [mid], parts, v, below, above, *statics, lines_z1)
     below, above = d.beside("py", v, v)
-    parts = d.solve_x(d.run(middle_scaled, [(4, MX, MZ)], v, below, above, *statics, keep=keep), rows_x)
-    v = d.run(gain_x, [mid], v, parts, keep=keep)
+    parts = d.solve_x(d.run(middle_scaled, [(4, MX, MZ)], v, below, above, *statics), rows_x)
+    v = d.run(gain_x, [mid], v, parts)
 
     below, above = d.beside("py", v, v)
     far_below, far_above = d.beside("py", v, v, 2)

time: 256 us -> 251 us (0.980)
  local copies, waits for them, and re-layouts: 17.4 us -> 10 us
  waiting for transfers between devices: 55.2 us -> 58.5 us
    unnamed x76 -> x70, local copies, waits for them, and re-layouts: 17.4 us -> 10 us
where the time goes in v1:
time: 251 us; the launch traced here: 249 us
  starting transfers between devices  86.9 us (35%)
  blocking collectives  80.4 us (32%)
  waiting for transfers between devices  58.5 us (23%)
  Pallas kernels  12.7 us (5%)
  local copies, waits for them, and re-layouts  10 us (4%)
    ppermute x18, starting transfers between devices, beside(): return (lax.ppermute(high, axis, up), lax.ppermute(low, axis, down))  55.9 us
    all_to_all x3, blocking collectives, swap(): lax.all_to_all(array, axis, 0, 0, axis_index_groups=groups, tiled=True)  55.2 us
    all_to_all x1, blocking collectives, solve_x(): lax.all_to_all(parts, 'px', 0, 0, axis_index_groups=eights, tiled=True)  25.2 us
    all_to_all x2, waiting for transfers between devices, swap(): lax.all_to_all(array, axis, 0, 0, axis_index_groups=groups, tiled=True)  20.8 us
    ppermute x18, waiting for transfers between devices, beside(): return (lax.ppermute(high, axis, up), lax.ppermute(low, axis, down))  19.9 us
    all_to_all x1, starting transfers between devices, everyone(): got = lax.all_to_all(sent, ('py', 'px'), 0, 0, tiled=True)  14.7 us
    pallas_call x20, Pallas kernels, run(): pl.pallas_call(kernel, out_shape=[jax.ShapeDtypeStruct(s, f32) for s in s...  12.7 us
    all_to_all x2, starting transfers between devices, swap(): lax.all_to_all(array, axis, 0, 0, axis_index_groups=groups, tiled=True)  12.3 us
  transfers between devices with their start and end apart: 23, of which 13 were waited for; matrix products, arithmetic and copies ran while one was open for 0% of the time, Pallas kernels for 1%

profile of v1, /device:TPU:8, one launch (start us, length us, event | category | flops | bytes accessed | tf_op | source)
XLA Modules:
  0.0 249.2 jit_solution(9988197744385031577)
XLA Ops:
  3.4 1.8 collective-permute-start
  5.2 1.3 collective-permute-start.1
  6.5 6.1 %collective-permute-start.2 = (f32[24,1024]{1,0:T(8,128)S(1)}, f32[24,1024]{1,0:T(8,128)S(1)}, u32[]{:S(2)}, u32[]{:S(2)}) collective-permute-start(f32[24,1024]{1,0:T(8,128)S(1)} %get-tuple-element.34), channel_id=1, source_target_pairs={{0,1},{1,2},{2,3},{3,4},{4,5},{5,6},{6,7},{7,8},{8,9},{9,10},{10,1... | collective-permute-start | bytes 294920 | tf_op jit(solution)/shard_map/ppermute | solution.py:558
  12.6 6.7 %collective-permute-start.3 = (f32[24,1024]{1,0:T(8,128)S(1)}, f32[24,1024]{1,0:T(8,128)S(1)}, u32[]{:S(2)}, u32[]{:S(2)}) collective-permute-start(f32[24,1024]{1,0:T(8,128)S(1)} %get-tuple-element.35), channel_id=1, source_target_pairs={{1,0},{2,1},{3,2},{4,3},{5,4},{6,5},{7,6},{8,7},{9,8},{10,9},{11,1... | collective-permute-start | bytes 294920 | tf_op jit(solution)/shard_map/ppermute | solution.py:558
  22.5 1.5 shard_map.102
  24.0 7.6 %all-to-all-start = ((f32[8,2,32,128]{3,2,1,0:T(8,128)}), f32[8,2,32,128]{3,2,1,0:T(8,128)S(1)}, u32[]{:S(2)}, u32[]{:S(2)}) async-start(f32[8,2,32,128]{3,2,1,0:T(8,128)} %shard_map.102), calls=%async_computation | async-start | bytes 524288 | tf_op jit(solution)/shard_map/all_to_all | solution.py:580
  31.6 11.2 %all-to-all-done.refs_0_ = f32[8,2,32,128]{3,2,1,0:T(8,128)S(1)} async-done(((f32[8,2,32,128]{3,2,1,0:T(8,128)}), f32[8,2,32,128]{3,2,1,0:T(8,128)S(1)}, u32[]{:S(2)}, u32[]{:S(2)}) %all-to-all-start) | async-done | bytes 262176 | tf_op jit(solution)/shard_map/all_to_all | solution.py:580
  43.9 4.7 %all-to-all-start.1 = ((f32[8,2,32,128]{3,2,1,0:T(8,128)}), f32[8,2,32,128]{3,2,1,0:T(8,128)S(1)}, u32[]{:S(2)}, u32[]{:S(2)}) async-start(f32[8,2,32,128]{3,2,1,0:T(8,128)} %shard_map.103), calls=%async_computation.1 | async-start | bytes 524288 | tf_op jit(solution)/shard_map/all_to_all | solution.py:580
  49.7 9.6 %all-to-all-done.1.refs_1_ = f32[8,2,32,128]{3,2,1,0:T(8,128)S(1)} async-done(((f32[8,2,32,128]{3,2,1,0:T(8,128)}), f32[8,2,32,128]{3,2,1,0:T(8,128)S(1)}, u32[]{:S(2)}, u32[]{:S(2)}) %all-to-all-start.1) | async-done | bytes 262176 | tf_op jit(solution)/shard_map/all_to_all | solution.py:580
  59.4 1.4 collective-permute-start.4
  62.1 4.3 %collective-permute-done.5.refs_2_.refs_3_ = f32[80,1024]{1,0:T(8,128)S(1)} collective-permute-done((f32[80,1024]{1,0:T(8,128)S(1)}, f32[80,1024]{1,0:T(8,128)S(1)}, u32[]{:S(2)}, u32[]{:S(2)}) %collective-permute-start.5) | collective-permute-done | bytes 327712 | tf_op jit(solution)/shard_map/ppermute | solution.py:558
  67.0 2.1 collective-permute-start.6
  69.2 6.7 %collective-permute-start.7 = (f32[24,1024]{1,0:T(8,128)S(1)}, f32[24,1024]{1,0:T(8,128)S(1)}, u32[]{:S(2)}, u32[]{:S(2)}) collective-permute-start(f32[24,1024]{1,0:T(8,128)S(1)} %get-tuple-element.39), channel_id=1, source_target_pairs={{1,0},{2,1},{3,2},{4,3},{5,4},{6,5},{7,6},{8,7},{9,8},{10,9},{11,1... | collective-permute-start | bytes 294920 | tf_op jit(solution)/shard_map/ppermute | solution.py:558
  76.6 1.5 collective-permute-done.7.refs_5_
  80.1 8.5 %collective-permute-start.8 = (f32[24,512]{1,0:T(8,128)S(1)}, f32[24,512]{1,0:T(8,128)S(1)}, u32[]{:S(2)}, u32[]{:S(2)}) collective-permute-start(f32[24,512]{1,0:T(8,128)S(1)} %get-tuple-element.42.refs_0_.refs_2_), channel_id=1, source_target_pairs={{0,32},{32,64},{64,96},{96,128},{128,160},{160,192},{192,224},{224... | collective-permute-start | bytes 147464 | tf_op jit(solution)/shard_map/ppermute | solution.py:558
  89.9 1.8 collective-permute-done.9.refs_2_
  91.9 27.4 %all_to_all.40 = f32[16,16,512]{2,1,0:T(8,128)S(1)} all-to-all(f32[16,16,512]{2,1,0:T(8,128)S(1)} %shard_map.108), channel_id=1, replica_groups={{0,1,2,3,4,5,6,7,8,9,10,11,12,13,14,15},{16,17,18,19,20,21,22,23,24,25,..., dimensions={0} | all-to-all | bytes 1048576 | tf_op jit(solution)/shard_map/all_to_all | solution.py:580
  121.0 14.7 %all-to-all-start.3 = ((f32[512,1,128]{2,1,0:T(1,128)}), f32[512,1,128]{2,1,0:T(1,128)S(1)}, u32[]{:S(2)}, u32[]{:S(2)}) async-start(f32[512,1,128]{2,1,0:T(1,128)} %bitcast.6), calls=%async_computation.3 | async-start | bytes 524288 | tf_op jit(solution)/shard_map/all_to_all | solution.py:565
  136.4 2.0 collective-permute-start.11
  139.8 3.2 %collective-permute-done.12.refs_3_ = f32[24,512]{1,0:T(8,128)S(1)} collective-permute-done((f32[24,512]{1,0:T(8,128)S(1)}, f32[24,512]{1,0:T(8,128)S(1)}, u32[]{:S(2)}, u32[]{:S(2)}) %collective-permute-start.12) | collective-permute-done | bytes 49184 | tf_op jit(solution)/shard_map/ppermute | solution.py:558
  143.0 9.5 %all-to-all-done.3 = f32[512,1,128]{2,1,0:T(1,128)S(1)} async-done(((f32[512,1,128]{2,1,0:T(1,128)}), f32[512,1,128]{2,1,0:T(1,128)S(1)}, u32[]{:S(2)}, u32[]{:S(2)}) %all-to-all-start.3) | async-done | bytes 262176 | tf_op jit(solution)/shard_map/all_to_all | solution.py:565
  156.4 3.1 %collective-permute-done.14.refs_2_ = f32[24,512]{1,0:T(8,128)S(1)} collective-permute-done((f32[24,512]{1,0:T(8,128)S(1)}, f32[24,512]{1,0:T(8,128)S(1)}, u32[]{:S(2)}, u32[]{:S(2)}) %collective-permute-start.14) | collective-permute-done | bytes 49184 | tf_op jit(solution)/shard_map/ppermute | solution.py:558
  160.3 3.3 %all-to-all-start.4 = ((f32[4,16,512]{2,1,0:T(8,128)}), f32[4,16,512]{2,1,0:T(8,128)S(1)}, u32[]{:S(2)}, u32[]{:S(2)}) async-start(f32[4,16,512]{2,1,0:T(8,128)} %shard_map.113), calls=%async_computation.4 | async-start | bytes 262144 | tf_op jit(solution)/shard_map/all_to_all | solution.py:571
  163.9 8.4 %all-to-all-done.4 = f32[4,16,512]{2,1,0:T(8,128)S(1)} async-done(((f32[4,16,512]{2,1,0:T(8,128)}), f32[4,16,512]{2,1,0:T(8,128)S(1)}, u32[]{:S(2)}, u32[]{:S(2)}) %all-to-all-start.4) | async-done | bytes 131104 | tf_op jit(solution)/shard_map/all_to_all | solution.py:571
  172.6 25.2 %all_to_all.41.refs_1_ = f32[8,24,512]{2,1,0:T(8,128)S(1)} all-to-all(f32[8,24,512]{2,1,0:T(8,128)S(1)} %shard_map.115), channel_id=1, replica_groups={{0,4,8,12,16,20,24,28},{1,5,9,13,17,21,25,29},{2,6,10,14,18,22,26,30},{..., dimensions={0} | all-to-all | bytes 786432 | tf_op jit(solution)/shard_map/all_to_all | solution.py:573
  197.8 2.5 %collective-permute-start.15 = (f32[24,512]{1,0:T(8,128)S(1)}, f32[24,512]{1,0:T(8,128)S(1)}, u32[]{:S(2)}, u32[]{:S(2)}) collective-permute-start(f32[24,512]{1,0:T(8,128)S(1)} %shard_map.116.refs_0_), channel_id=1, source_target_pairs={{0,32},{32,64},{64,96},{96,128},{128,160},{160,192},{192,224},{224... | collective-permute-start | bytes 147464 | tf_op jit(solution)/shard_map/ppermute | solution.py:558
  201.6 7.5 %collective-permute-start.17 = (f32[24,512]{1,0:T(8,128)S(1)}, f32[24,512]{1,0:T(8,128)S(1)}, u32[]{:S(2)}, u32[]{:S(2)}) collective-permute-start(f32[24,512]{1,0:T(8,128)S(1)} %shard_map.116.refs_0_), channel_id=1, source_target_pairs={{0,64},{32,96},{64,128},{96,160},{128,192},{160,224},{192,256},{22... | collective-permute-start | bytes 147464 | tf_op jit(solution)/shard_map/ppermute | solution.py:558
  209.1 1.5 collective-permute-start.18
  210.9 4.3 %collective-permute-done.18.refs_4_ = f32[24,512]{1,0:T(8,128)S(1)} collective-permute-done((f32[24,512]{1,0:T(8,128)S(1)}, f32[24,512]{1,0:T(8,128)S(1)}, u32[]{:S(2)}, u32[]{:S(2)}) %collective-permute-start.18) | collective-permute-done | bytes 49184 | tf_op jit(solution)/shard_map/ppermute | solution.py:558
  217.5 2.7 %shard_map.117 = (f32[2,32,1024]{2,1,0:T(8,128)S(1)}, f32[8,2,32,128]{3,2,1,0:T(8,128)S(1)}) custom-call(f32[24,512]{1,0:T(8,128)S(1)} %shard_map.116.refs_0_, f32[24,512]{1,0:T(8,128)S(1)} %collective-permute-done.15.refs_1_, f32[24,512]{1,0:T(8,128)S(1)} %collective-permute-done.16.refs_2_, f32[24,512]{1,0:T(8,128)S(1)} %collective-permute-done.17.refs_3_, ...), custom_call_target="tpu_custom_call" | custom-call | tf_op jit(solution)/shard_map/pallas_call | solution.py:538
  220.3 13.6 %all_to_all.42.refs_0_ = f32[8,2,32,128]{3,2,1,0:T(8,128)S(1)} all-to-all(f32[8,2,32,128]{3,2,1,0:T(8,128)S(1)} %get-tuple-element.52), channel_id=1, replica_groups={{0,1,2,3,4,5,6,7},{8,9,10,11,12,13,14,15},{16,17,18,19,20,21,22,23},{24..., dimensions={0} | all-to-all | bytes 524288 | tf_op jit(solution)/shard_map/all_to_all | solution.py:580
  234.3 14.1 %all_to_all.43.refs_1_ = f32[8,2,32,128]{3,2,1,0:T(8,128)S(1)} all-to-all(f32[8,2,32,128]{3,2,1,0:T(8,128)S(1)} %shard_map.118), channel_id=1, replica_groups={{0,1,2,3,4,5,6,7},{8,9,10,11,12,13,14,15},{16,17,18,19,20,21,22,23},{24..., dimensions={0} | all-to-all | bytes 524288 | tf_op jit(solution)/shard_map/all_to_all | solution.py:580
  (109 shorter events, 28.5 us)
Async XLA Ops:
  3.4 19.1 %collective-permute-start = (f32[72,1024]{1,0:T(8,128)S(1)}, f32[72,1024]{1,0:T(8,128)S(1)}, u32[]{:S(2)}, u32[]{:S(2)}) collective-permute-start(f32[72,1024]{1,0:T(8,128)S(1)} %get-tuple-element.32), channel_id=1, source_target_pairs={{0,32},{32,64},{64,96},{96,128},{128,160},{160,192},{192,224},{224... | collective-permute-start | bytes 884744 | tf_op jit(solution)/shard_map/ppermute | solution.py:558
  5.2 17.3 %collective-permute-start.1 = (f32[72,1024]{1,0:T(8,128)S(1)}, f32[72,1024]{1,0:T(8,128)S(1)}, u32[]{:S(2)}, u32[]{:S(2)}) collective-permute-start(f32[72,1024]{1,0:T(8,128)S(1)} %get-tuple-element.33), channel_id=1, source_target_pairs={{32,0},{64,32},{96,64},{128,96},{160,128},{192,160},{224,192},{256... | collective-permute-start | bytes 884744 | tf_op jit(solution)/shard_map/ppermute | solution.py:558
  6.5 15.3 %collective-permute-start.2 = (f32[24,1024]{1,0:T(8,128)S(1)}, f32[24,1024]{1,0:T(8,128)S(1)}, u32[]{:S(2)}, u32[]{:S(2)}) collective-permute-start(f32[24,1024]{1,0:T(8,128)S(1)} %get-tuple-element.34), channel_id=1, source_target_pairs={{0,1},{1,2},{2,3},{3,4},{4,5},{5,6},{6,7},{7,8},{8,9},{9,10},{10,1... | collective-permute-start | bytes 294920 | tf_op jit(solution)/shard_map/ppermute | solution.py:558
  12.6 9.9 %collective-permute-start.3 = (f32[24,1024]{1,0:T(8,128)S(1)}, f32[24,1024]{1,0:T(8,128)S(1)}, u32[]{:S(2)}, u32[]{:S(2)}) collective-permute-start(f32[24,1024]{1,0:T(8,128)S(1)} %get-tuple-element.35), channel_id=1, source_target_pairs={{1,0},{2,1},{3,2},{4,3},{5,4},{6,5},{7,6},{8,7},{9,8},{10,9},{11,1... | collective-permute-start | bytes 294920 | tf_op jit(solution)/shard_map/ppermute | solution.py:558
  24.0 18.8 %all-to-all-start = ((f32[8,2,32,128]{3,2,1,0:T(8,128)}), f32[8,2,32,128]{3,2,1,0:T(8,128)S(1)}, u32[]{:S(2)}, u32[]{:S(2)}) async-start(f32[8,2,32,128]{3,2,1,0:T(8,128)} %shard_map.102), calls=%async_computation | async-start | bytes 524288 | tf_op jit(solution)/shard_map/all_to_all | solution.py:580
  43.9 15.4 %all-to-all-start.1 = ((f32[8,2,32,128]{3,2,1,0:T(8,128)}), f32[8,2,32,128]{3,2,1,0:T(8,128)S(1)}, u32[]{:S(2)}, u32[]{:S(2)}) async-start(f32[8,2,32,128]{3,2,1,0:T(8,128)} %shard_map.103), calls=%async_computation.1 | async-start | bytes 524288 | tf_op jit(solution)/shard_map/all_to_all | solution.py:580
  59.4 2.8 %collective-permute-start.4 = (f32[80,1024]{1,0:T(8,128)S(1)}, f32[80,1024]{1,0:T(8,128)S(1)}, u32[]{:S(2)}, u32[]{:S(2)}) collective-permute-start(f32[80,1024]{1,0:T(8,128)S(1)} %shard_map.105.refs_0_.refs_1_), channel_id=1, source_target_pairs={{0,32},{32,64},{64,96},{96,128},{128,160},{160,192},{192,224},{224... | collective-permute-start | bytes 983048 | tf_op jit(solution)/shard_map/ppermute | solution.py:558
  60.8 5.6 %collective-permute-start.5 = (f32[80,1024]{1,0:T(8,128)S(1)}, f32[80,1024]{1,0:T(8,128)S(1)}, u32[]{:S(2)}, u32[]{:S(2)}) collective-permute-start(f32[80,1024]{1,0:T(8,128)S(1)} %shard_map.105.refs_0_.refs_1_), channel_id=1, source_target_pairs={{32,0},{64,32},{96,64},{128,96},{160,128},{192,160},{224,192},{256... | collective-permute-start | bytes 983048 | tf_op jit(solution)/shard_map/ppermute | solution.py:558
  67.0 9.5 %collective-permute-start.6 = (f32[24,1024]{1,0:T(8,128)S(1)}, f32[24,1024]{1,0:T(8,128)S(1)}, u32[]{:S(2)}, u32[]{:S(2)}) collective-permute-start(f32[24,1024]{1,0:T(8,128)S(1)} %get-tuple-element.38), channel_id=1, source_target_pairs={{0,1},{1,2},{2,3},{3,4},{4,5},{5,6},{6,7},{7,8},{8,9},{9,10},{10,1... | collective-permute-start | bytes 294920 | tf_op jit(solution)/shard_map/ppermute | solution.py:558
  69.2 8.9 %collective-permute-start.7 = (f32[24,1024]{1,0:T(8,128)S(1)}, f32[24,1024]{1,0:T(8,128)S(1)}, u32[]{:S(2)}, u32[]{:S(2)}) collective-permute-start(f32[24,1024]{1,0:T(8,128)S(1)} %get-tuple-element.39), channel_id=1, source_target_pairs={{1,0},{2,1},{3,2},{4,3},{5,4},{6,5},{7,6},{8,7},{9,8},{10,9},{11,1... | collective-permute-start | bytes 294920 | tf_op jit(solution)/shard_map/ppermute | solution.py:558
  80.1 39.6 %copy-start.15 = (f32[4,48,1024]{2,1,0:T(8,128)}, f32[4,48,1024]{2,1,0:T(8,128)S(1)}, u32[]{:S(2)}) copy-start(f32[4,48,1024]{2,1,0:T(8,128)S(1)} %get-tuple-element.48.refs_7_) | copy-start | bytes 2359300
  80.1 39.6 %copy-start.25 = (f32[8,1024]{1,0:T(8,128)}, f32[8,1024]{1,0:T(8,128)S(1)}, u32[]{:S(2)}) copy-start(f32[8,1024]{1,0:T(8,128)S(1)} %get-tuple-element.50.refs_9_) | copy-start | bytes 98308
  80.1 39.6 %copy-start.27 = (f32[48,128]{1,0:T(8,128)}, f32[48,128]{1,0:T(8,128)S(1)}, u32[]{:S(2)}) copy-start(f32[48,128]{1,0:T(8,128)S(1)} %get-tuple-element.49.refs_8_) | copy-start | bytes 73732
  80.1 39.6 %copy-start.11 = (f32[24,512]{1,0:T(8,128)}, f32[24,512]{1,0:T(8,128)S(1)}, u32[]{:S(2)}) copy-start(f32[24,512]{1,0:T(8,128)S(1)} %get-tuple-element.43.refs_3_.refs_1_.refs_4_) | copy-start | bytes 147460
  80.1 9.8 %collective-permute-start.8 = (f32[24,512]{1,0:T(8,128)S(1)}, f32[24,512]{1,0:T(8,128)S(1)}, u32[]{:S(2)}, u32[]{:S(2)}) collective-permute-start(f32[24,512]{1,0:T(8,128)S(1)} %get-tuple-element.42.refs_0_.refs_2_), channel_id=1, source_target_pairs={{0,32},{32,64},{64,96},{96,128},{128,160},{160,192},{192,224},{224... | collective-permute-start | bytes 147464 | tf_op jit(solution)/shard_map/ppermute | solution.py:558
  88.6 3.1 %collective-permute-start.9 = (f32[24,512]{1,0:T(8,128)S(1)}, f32[24,512]{1,0:T(8,128)S(1)}, u32[]{:S(2)}, u32[]{:S(2)}) collective-permute-start(f32[24,512]{1,0:T(8,128)S(1)} %get-tuple-element.42.refs_0_.refs_2_), channel_id=1, source_target_pairs={{32,0},{64,32},{96,64},{128,96},{160,128},{192,160},{224,192},{256... | collective-permute-start | bytes 147464 | tf_op jit(solution)/shard_map/ppermute | solution.py:558
  121.0 31.5 %all-to-all-start.3 = ((f32[512,1,128]{2,1,0:T(1,128)}), f32[512,1,128]{2,1,0:T(1,128)S(1)}, u32[]{:S(2)}, u32[]{:S(2)}) async-start(f32[512,1,128]{2,1,0:T(1,128)} %bitcast.6), calls=%async_computation.3 | async-start | bytes 524288 | tf_op jit(solution)/shard_map/all_to_all | solution.py:565
  135.7 0.7 collective-permute-start.10
  136.4 3.3 %collective-permute-start.11 = (f32[24,512]{1,0:T(8,128)S(1)}, f32[24,512]{1,0:T(8,128)S(1)}, u32[]{:S(2)}, u32[]{:S(2)}) collective-permute-start(f32[24,512]{1,0:T(8,128)S(1)} %shard_map.111.refs_1_), channel_id=1, source_target_pairs={{0,32},{32,64},{64,96},{96,128},{128,160},{160,192},{192,224},{224... | collective-permute-start | bytes 147464 | tf_op jit(solution)/shard_map/ppermute | solution.py:558
  138.4 4.5 %collective-permute-start.12 = (f32[24,512]{1,0:T(8,128)S(1)}, f32[24,512]{1,0:T(8,128)S(1)}, u32[]{:S(2)}, u32[]{:S(2)}) collective-permute-start(f32[24,512]{1,0:T(8,128)S(1)} %shard_map.111.refs_1_), channel_id=1, source_target_pairs={{32,0},{64,32},{96,64},{128,96},{160,128},{192,160},{224,192},{256... | collective-permute-start | bytes 147464 | tf_op jit(solution)/shard_map/ppermute | solution.py:558
  153.8 2.6 %collective-permute-start.13 = (f32[24,512]{1,0:T(8,128)S(1)}, f32[24,512]{1,0:T(8,128)S(1)}, u32[]{:S(2)}, u32[]{:S(2)}) collective-permute-start(f32[24,512]{1,0:T(8,128)S(1)} %shard_map.112.refs_0_), channel_id=1, source_target_pairs={{0,32},{32,64},{64,96},{96,128},{128,160},{160,192},{192,224},{224... | collective-permute-start | bytes 147464 | tf_op jit(solution)/shard_map/ppermute | solution.py:558
  155.1 4.5 %collective-permute-start.14 = (f32[24,512]{1,0:T(8,128)S(1)}, f32[24,512]{1,0:T(8,128)S(1)}, u32[]{:S(2)}, u32[]{:S(2)}) collective-permute-start(f32[24,512]{1,0:T(8,128)S(1)} %shard_map.112.refs_0_), channel_id=1, source_target_pairs={{32,0},{64,32},{96,64},{128,96},{160,128},{192,160},{224,192},{256... | collective-permute-start | bytes 147464 | tf_op jit(solution)/shard_map/ppermute | solution.py:558
  160.3 12.0 %all-to-all-start.4 = ((f32[4,16,512]{2,1,0:T(8,128)}), f32[4,16,512]{2,1,0:T(8,128)S(1)}, u32[]{:S(2)}, u32[]{:S(2)}) async-start(f32[4,16,512]{2,1,0:T(8,128)} %shard_map.113), calls=%async_computation.4 | async-start | bytes 262144 | tf_op jit(solution)/shard_map/all_to_all | solution.py:571
  163.7 51.4 %copy-start.2 = (f32[4,256,256]{2,1,0:T(8,128)S(1)}, f32[4,256,256]{2,1,0:T(8,128)}, u32[]{:S(2)}) copy-start(f32[4,256,256]{2,1,0:T(8,128)} %refs_11_.1) | copy-start | bytes 3145732
  163.7 51.4 %copy-start.24 = (f32[1024]{0:T(1024)S(1)}, f32[1024]{0:T(1024)}, u32[]{:S(2)}) copy-start(f32[1024]{0:T(1024)} %param.14) | copy-start | bytes 12292
  163.7 51.4 %copy-start.26 = (f32[8,1024]{1,0:T(8,128)S(1)}, f32[8,1024]{1,0:T(8,128)}, u32[]{:S(2)}) copy-start(f32[8,1024]{1,0:T(8,128)} %copy-done.25) | copy-start | bytes 98308
  163.7 51.4 %copy-start.28 = (f32[48,128]{1,0:T(8,128)S(1)}, f32[48,128]{1,0:T(8,128)}, u32[]{:S(2)}) copy-start(f32[48,128]{1,0:T(8,128)} %copy-done.27) | copy-start | bytes 73732
  163.9 51.2 %copy-start.14 = (f32[4,48,1024]{2,1,0:T(8,128)S(1)}, f32[4,48,1024]{2,1,0:T(8,128)}, u32[]{:S(2)}) copy-start(f32[4,48,1024]{2,1,0:T(8,128)} %copy-done.13) | copy-start | bytes 2359300
  197.8 12.8 %collective-permute-start.15 = (f32[24,512]{1,0:T(8,128)S(1)}, f32[24,512]{1,0:T(8,128)S(1)}, u32[]{:S(2)}, u32[]{:S(2)}) collective-permute-start(f32[24,512]{1,0:T(8,128)S(1)} %shard_map.116.refs_0_), channel_id=1, source_target_pairs={{0,32},{32,64},{64,96},{96,128},{128,160},{160,192},{192,224},{224... | collective-permute-start | bytes 147464 | tf_op jit(solution)/shard_map/ppermute | solution.py:558
  200.3 10.3 %collective-permute-start.16 = (f32[24,512]{1,0:T(8,128)S(1)}, f32[24,512]{1,0:T(8,128)S(1)}, u32[]{:S(2)}, u32[]{:S(2)}) collective-permute-start(f32[24,512]{1,0:T(8,128)S(1)} %shard_map.116.refs_0_), channel_id=1, source_target_pairs={{32,0},{64,32},{96,64},{128,96},{160,128},{192,160},{224,192},{256... | collective-permute-start | bytes 147464 | tf_op jit(solution)/shard_map/ppermute | solution.py:558
  201.6 9.2 %collective-permute-start.17 = (f32[24,512]{1,0:T(8,128)S(1)}, f32[24,512]{1,0:T(8,128)S(1)}, u32[]{:S(2)}, u32[]{:S(2)}) collective-permute-start(f32[24,512]{1,0:T(8,128)S(1)} %shard_map.116.refs_0_), channel_id=1, source_target_pairs={{0,64},{32,96},{64,128},{96,160},{128,192},{160,224},{192,256},{22... | collective-permute-start | bytes 147464 | tf_op jit(solution)/shard_map/ppermute | solution.py:558
  209.1 6.0 %collective-permute-start.18 = (f32[24,512]{1,0:T(8,128)S(1)}, f32[24,512]{1,0:T(8,128)S(1)}, u32[]{:S(2)}, u32[]{:S(2)}) collective-permute-start(f32[24,512]{1,0:T(8,128)S(1)} %shard_map.116.refs_0_), channel_id=1, source_target_pairs={{64,0},{96,32},{128,64},{160,96},{192,128},{224,160},{256,192},{28... | collective-permute-start | bytes 147464 | tf_op jit(solution)/shard_map/ppermute | solution.py:558
  (26 other events, 401.7 us)

commit v2 on v1

--- a/solution.py
+++ b/solution.py
@@ -192,9 +192,9 @@
     return jnp.concatenate([ref[m, at] for m in range(8)], axis=1)
 
 
-def start(px, py, forcing, inv_density, sx, sy, force, rho, lower, upper, low, high, cx):
+def start(px, py, forcing, inv_density, sxy, force, rho, lower, upper, low, high, cx):
     square = iota((FX, FX), 0) == iota((FX, FX), 1)
-    column = jnp.sum(jnp.where(square, sx[...], 0.0), axis=1, keepdims=True)
+    column = jnp.sum(jnp.where(square, sxy[0:1, 0:FX], 0.0), axis=1, keepdims=True)
     cx[...] = jnp.broadcast_to(column, (FX, 128))
     wide = jnp.broadcast_to(column, (FX, FZ))
     edges = {}
@@ -204,7 +204,7 @@
         rho[at] = r_plane
         out[0:32] = f_plane
         out[32:64] = r_plane
-        out[64:72] = jnp.broadcast_to(sy[0:1, at : at + 1], (8, FZ))
+        out[64:72] = jnp.broadcast_to(sxy[0:1, FX + at : FX + at + 1], (8, FZ))
         for row in (0, FX - 1):
             edges[at, row] = (f_plane[row : row + 1], r_plane[row : row + 1])
     for side, row, cut in ((low, 0, slice(0, 8)), (high, FX - 1, slice(24, 32))):
@@ -530,7 +530,7 @@
 
 
 class Device:
-    def run(self, stage, shapes, *args, grant=24):
+    def run(self, stage, shapes, *args):
         def kernel(*refs):
             stage(lax.axis_index("px"), lax.axis_index("py"), *refs)
 
@@ -540,7 +540,7 @@
             out_shape=[jax.ShapeDtypeStruct(s, f32) for s in shapes],
             in_specs=[whole] * len(args),
             out_specs=[whole] * len(shapes),
-            compiler_params=pltpu.CompilerParams(vmem_limit_bytes=grant * 1024 * 1024),
+            compiler_params=pltpu.CompilerParams(vmem_limit_bytes=24 * 1024 * 1024),
         )(*args)
         return outs if len(shapes) > 1 else outs[0]
 
@@ -581,7 +581,7 @@
 
 
 def cycle(d, forcing, inv_density, stretch_x, stretch_y, stretch_z, lines_z0, lines_x0, lines_z1, lines_x1, column):
-    sx = d.local(lambda a: a.reshape(1, FX), stretch_x)
+    sxy = d.local(lambda a, b: jnp.concatenate([a, b])[None], stretch_x, stretch_y)
     sy = d.local(lambda a: a.reshape(1, 2), stretch_y)
     cz = d.local(lambda a: a.reshape(1, FZ), stretch_z)
     rows_x1 = d.local(lambda a: a.reshape(MX * N_PX, 256), lines_x1)
@@ -590,7 +590,7 @@
     force, rho, lower, upper, low, high, cx = d.run(
         start,
         [own, own, (72, FZ), (72, FZ), (24, FZ), (24, FZ), (FX, 128)],
-        forcing, inv_density, sx, sy,
+        forcing, inv_density, sxy,
     )
     y_below, y_above = d.beside("py", lower, upper)
     x_left, x_right = d.beside("px", low, high)

time: 251 us -> 250 us (level)
    unnamed x70 -> x68, local copies, waits for them, and re-layouts: 10 us -> 9.28 us
  transfers between devices with their start and end apart: 23 -> 23, of which waited for: 13 -> 12; matrix products, arithmetic and copies ran while one was open for 0% -> 0% of each run, Pallas kernels for 1% -> 1%
where the time goes in v2:
time: 250 us; the launch traced here: 249 us
  starting transfers between devices  87.8 us (35%)
  blocking collectives  80.8 us (32%)
  waiting for transfers between devices  56.6 us (23%)
  Pallas kernels  12.7 us (5%)
  local copies, waits for them, and re-layouts  9.29 us (4%)
    ppermute x18, starting transfers between devices, beside(): return (lax.ppermute(high, axis, up), lax.ppermute(low, axis, down))  55.8 us
    all_to_all x3, blocking collectives, swap(): lax.all_to_all(array, axis, 0, 0, axis_index_groups=groups, tiled=True)  55.6 us
    all_to_all x1, blocking collectives, solve_x(): lax.all_to_all(parts, 'px', 0, 0, axis_index_groups=eights, tiled=True)  25.1 us
    ppermute x18, waiting for transfers between devices, beside(): return (lax.ppermute(high, axis, up), lax.ppermute(low, axis, down))  19.4 us
    all_to_all x2, waiting for transfers between devices, swap(): lax.all_to_all(array, axis, 0, 0, axis_index_groups=groups, tiled=True)  19.3 us
    all_to_all x1, starting transfers between devices, everyone(): got = lax.all_to_all(sent, ('py', 'px'), 0, 0, tiled=True)  14.3 us
    all_to_all x2, starting transfers between devices, swap(): lax.all_to_all(array, axis, 0, 0, axis_index_groups=groups, tiled=True)  13.7 us
    pallas_call x20, Pallas kernels, run(): pl.pallas_call(kernel, out_shape=[jax.ShapeDtypeStruct(s, f32) for s in s...  12.7 us
  transfers between devices with their start and end apart: 23, of which 12 were waited for; matrix products, arithmetic and copies ran while one was open for 0% of the time, Pallas kernels for 1%

profile of v2, /device:TPU:8, one launch (start us, length us, event | category | flops | bytes accessed | tf_op | source)
XLA Modules:
  0.0 248.6 jit_solution(16042824589855446144)
XLA Ops:
  2.9 1.8 collective-permute-start
  5.9 6.1 %collective-permute-start.2 = (f32[24,1024]{1,0:T(8,128)S(1)}, f32[24,1024]{1,0:T(8,128)S(1)}, u32[]{:S(2)}, u32[]{:S(2)}) collective-permute-start(f32[24,1024]{1,0:T(8,128)S(1)} %get-tuple-element.34), channel_id=1, source_target_pairs={{0,1},{1,2},{2,3},{3,4},{4,5},{5,6},{6,7},{7,8},{8,9},{9,10},{10,1... | collective-permute-start | bytes 294920 | tf_op jit(solution)/shard_map/ppermute | solution.py:558
  12.0 6.7 %collective-permute-start.3 = (f32[24,1024]{1,0:T(8,128)S(1)}, f32[24,1024]{1,0:T(8,128)S(1)}, u32[]{:S(2)}, u32[]{:S(2)}) collective-permute-start(f32[24,1024]{1,0:T(8,128)S(1)} %get-tuple-element.35), channel_id=1, source_target_pairs={{1,0},{2,1},{3,2},{4,3},{5,4},{6,5},{7,6},{8,7},{9,8},{10,9},{11,1... | collective-permute-start | bytes 294920 | tf_op jit(solution)/shard_map/ppermute | solution.py:558
  22.0 1.5 shard_map.102
  23.5 7.5 %all-to-all-start = ((f32[8,2,32,128]{3,2,1,0:T(8,128)}), f32[8,2,32,128]{3,2,1,0:T(8,128)S(1)}, u32[]{:S(2)}, u32[]{:S(2)}) async-start(f32[8,2,32,128]{3,2,1,0:T(8,128)} %shard_map.102), calls=%async_computation | async-start | bytes 524288 | tf_op jit(solution)/shard_map/all_to_all | solution.py:580
  31.1 9.8 %all-to-all-done.refs_0_ = f32[8,2,32,128]{3,2,1,0:T(8,128)S(1)} async-done(((f32[8,2,32,128]{3,2,1,0:T(8,128)}), f32[8,2,32,128]{3,2,1,0:T(8,128)S(1)}, u32[]{:S(2)}, u32[]{:S(2)}) %all-to-all-start) | async-done | bytes 262176 | tf_op jit(solution)/shard_map/all_to_all | solution.py:580
  41.9 6.1 %all-to-all-start.1 = ((f32[8,2,32,128]{3,2,1,0:T(8,128)}), f32[8,2,32,128]{3,2,1,0:T(8,128)S(1)}, u32[]{:S(2)}, u32[]{:S(2)}) async-start(f32[8,2,32,128]{3,2,1,0:T(8,128)} %shard_map.103), calls=%async_computation.1 | async-start | bytes 524288 | tf_op jit(solution)/shard_map/all_to_all | solution.py:580
  49.2 9.5 %all-to-all-done.1.refs_1_ = f32[8,2,32,128]{3,2,1,0:T(8,128)S(1)} async-done(((f32[8,2,32,128]{3,2,1,0:T(8,128)}), f32[8,2,32,128]{3,2,1,0:T(8,128)S(1)}, u32[]{:S(2)}, u32[]{:S(2)}) %all-to-all-start.1) | async-done | bytes 262176 | tf_op jit(solution)/shard_map/all_to_all | solution.py:580
  58.8 1.4 collective-permute-start.4
  60.2 1.3 collective-permute-start.5
  61.5 4.5 %collective-permute-done.5.refs_2_.refs_3_ = f32[80,1024]{1,0:T(8,128)S(1)} collective-permute-done((f32[80,1024]{1,0:T(8,128)S(1)}, f32[80,1024]{1,0:T(8,128)S(1)}, u32[]{:S(2)}, u32[]{:S(2)}) %collective-permute-start.5) | collective-permute-done | bytes 327712 | tf_op jit(solution)/shard_map/ppermute | solution.py:558
  66.6 2.1 collective-permute-start.6
  68.7 6.8 %collective-permute-start.7 = (f32[24,1024]{1,0:T(8,128)S(1)}, f32[24,1024]{1,0:T(8,128)S(1)}, u32[]{:S(2)}, u32[]{:S(2)}) collective-permute-start(f32[24,1024]{1,0:T(8,128)S(1)} %get-tuple-element.39), channel_id=1, source_target_pairs={{1,0},{2,1},{3,2},{4,3},{5,4},{6,5},{7,6},{8,7},{9,8},{10,9},{11,1... | collective-permute-start | bytes 294920 | tf_op jit(solution)/shard_map/ppermute | solution.py:558
  76.1 1.5 collective-permute-done.7.refs_5_
  79.6 8.4 %collective-permute-start.8 = (f32[24,512]{1,0:T(8,128)S(1)}, f32[24,512]{1,0:T(8,128)S(1)}, u32[]{:S(2)}, u32[]{:S(2)}) collective-permute-start(f32[24,512]{1,0:T(8,128)S(1)} %get-tuple-element.42.refs_0_.refs_2_), channel_id=1, source_target_pairs={{0,32},{32,64},{64,96},{96,128},{128,160},{160,192},{192,224},{224... | collective-permute-start | bytes 147464 | tf_op jit(solution)/shard_map/ppermute | solution.py:558
  89.4 1.8 collective-permute-done.9.refs_2_
  91.4 27.8 %all_to_all.40 = f32[16,16,512]{2,1,0:T(8,128)S(1)} all-to-all(f32[16,16,512]{2,1,0:T(8,128)S(1)} %shard_map.108), channel_id=1, replica_groups={{0,1,2,3,4,5,6,7,8,9,10,11,12,13,14,15},{16,17,18,19,20,21,22,23,24,25,..., dimensions={0} | all-to-all | bytes 1048576 | tf_op jit(solution)/shard_map/all_to_all | solution.py:580
  120.8 14.3 %all-to-all-start.3 = ((f32[512,1,128]{2,1,0:T(1,128)}), f32[512,1,128]{2,1,0:T(1,128)S(1)}, u32[]{:S(2)}, u32[]{:S(2)}) async-start(f32[512,1,128]{2,1,0:T(1,128)} %bitcast.6), calls=%async_computation.3 | async-start | bytes 524288 | tf_op jit(solution)/shard_map/all_to_all | solution.py:565
  135.8 2.0 collective-permute-start.11
  139.2 3.2 %collective-permute-done.12.refs_3_ = f32[24,512]{1,0:T(8,128)S(1)} collective-permute-done((f32[24,512]{1,0:T(8,128)S(1)}, f32[24,512]{1,0:T(8,128)S(1)}, u32[]{:S(2)}, u32[]{:S(2)}) %collective-permute-start.12) | collective-permute-done | bytes 49184 | tf_op jit(solution)/shard_map/ppermute | solution.py:558
  142.4 9.5 %all-to-all-done.3 = f32[512,1,128]{2,1,0:T(1,128)S(1)} async-done(((f32[512,1,128]{2,1,0:T(1,128)}), f32[512,1,128]{2,1,0:T(1,128)S(1)}, u32[]{:S(2)}, u32[]{:S(2)}) %all-to-all-start.3) | async-done | bytes 262176 | tf_op jit(solution)/shard_map/all_to_all | solution.py:565
  155.8 3.2 %collective-permute-done.14.refs_2_ = f32[24,512]{1,0:T(8,128)S(1)} collective-permute-done((f32[24,512]{1,0:T(8,128)S(1)}, f32[24,512]{1,0:T(8,128)S(1)}, u32[]{:S(2)}, u32[]{:S(2)}) %collective-permute-start.14) | collective-permute-done | bytes 49184 | tf_op jit(solution)/shard_map/ppermute | solution.py:558
  159.8 3.3 %all-to-all-start.4 = ((f32[4,16,512]{2,1,0:T(8,128)}), f32[4,16,512]{2,1,0:T(8,128)S(1)}, u32[]{:S(2)}, u32[]{:S(2)}) async-start(f32[4,16,512]{2,1,0:T(8,128)} %shard_map.113), calls=%async_computation.4 | async-start | bytes 262144 | tf_op jit(solution)/shard_map/all_to_all | solution.py:571
  163.3 8.4 %all-to-all-done.4 = f32[4,16,512]{2,1,0:T(8,128)S(1)} async-done(((f32[4,16,512]{2,1,0:T(8,128)}), f32[4,16,512]{2,1,0:T(8,128)S(1)}, u32[]{:S(2)}, u32[]{:S(2)}) %all-to-all-start.4) | async-done | bytes 131104 | tf_op jit(solution)/shard_map/all_to_all | solution.py:571
  172.0 25.1 %all_to_all.41.refs_1_ = f32[8,24,512]{2,1,0:T(8,128)S(1)} all-to-all(f32[8,24,512]{2,1,0:T(8,128)S(1)} %shard_map.115), channel_id=1, replica_groups={{0,4,8,12,16,20,24,28},{1,5,9,13,17,21,25,29},{2,6,10,14,18,22,26,30},{..., dimensions={0} | all-to-all | bytes 786432 | tf_op jit(solution)/shard_map/all_to_all | solution.py:573
  197.2 2.5 %collective-permute-start.15 = (f32[24,512]{1,0:T(8,128)S(1)}, f32[24,512]{1,0:T(8,128)S(1)}, u32[]{:S(2)}, u32[]{:S(2)}) collective-permute-start(f32[24,512]{1,0:T(8,128)S(1)} %shard_map.116.refs_0_), channel_id=1, source_target_pairs={{0,32},{32,64},{64,96},{96,128},{128,160},{160,192},{192,224},{224... | collective-permute-start | bytes 147464 | tf_op jit(solution)/shard_map/ppermute | solution.py:558
  201.0 7.5 %collective-permute-start.17 = (f32[24,512]{1,0:T(8,128)S(1)}, f32[24,512]{1,0:T(8,128)S(1)}, u32[]{:S(2)}, u32[]{:S(2)}) collective-permute-start(f32[24,512]{1,0:T(8,128)S(1)} %shard_map.116.refs_0_), channel_id=1, source_target_pairs={{0,64},{32,96},{64,128},{96,160},{128,192},{160,224},{192,256},{22... | collective-permute-start | bytes 147464 | tf_op jit(solution)/shard_map/ppermute | solution.py:558
  208.5 1.5 collective-permute-start.18
  210.3 4.3 %collective-permute-done.18.refs_4_ = f32[24,512]{1,0:T(8,128)S(1)} collective-permute-done((f32[24,512]{1,0:T(8,128)S(1)}, f32[24,512]{1,0:T(8,128)S(1)}, u32[]{:S(2)}, u32[]{:S(2)}) %collective-permute-start.18) | collective-permute-done | bytes 49184 | tf_op jit(solution)/shard_map/ppermute | solution.py:558
  217.0 2.7 %shard_map.117 = (f32[2,32,1024]{2,1,0:T(8,128)S(1)}, f32[8,2,32,128]{3,2,1,0:T(8,128)S(1)}) custom-call(f32[24,512]{1,0:T(8,128)S(1)} %shard_map.116.refs_0_, f32[24,512]{1,0:T(8,128)S(1)} %collective-permute-done.15.refs_1_, f32[24,512]{1,0:T(8,128)S(1)} %collective-permute-done.16.refs_2_, f32[24,512]{1,0:T(8,128)S(1)} %collective-permute-done.17.refs_3_, ...), custom_call_target="tpu_custom_call" | custom-call | tf_op jit(solution)/shard_map/pallas_call | solution.py:538
  219.7 13.6 %all_to_all.42.refs_0_ = f32[8,2,32,128]{3,2,1,0:T(8,128)S(1)} all-to-all(f32[8,2,32,128]{3,2,1,0:T(8,128)S(1)} %get-tuple-element.52), channel_id=1, replica_groups={{0,1,2,3,4,5,6,7},{8,9,10,11,12,13,14,15},{16,17,18,19,20,21,22,23},{24..., dimensions={0} | all-to-all | bytes 524288 | tf_op jit(solution)/shard_map/all_to_all | solution.py:580
  233.7 14.2 %all_to_all.43.refs_1_ = f32[8,2,32,128]{3,2,1,0:T(8,128)S(1)} all-to-all(f32[8,2,32,128]{3,2,1,0:T(8,128)S(1)} %shard_map.118), channel_id=1, replica_groups={{0,1,2,3,4,5,6,7},{8,9,10,11,12,13,14,15},{16,17,18,19,20,21,22,23},{24..., dimensions={0} | all-to-all | bytes 524288 | tf_op jit(solution)/shard_map/all_to_all | solution.py:580
  (108 shorter events, 28.0 us)
Async XLA Ops:
  2.9 19.1 %collective-permute-start = (f32[72,1024]{1,0:T(8,128)S(1)}, f32[72,1024]{1,0:T(8,128)S(1)}, u32[]{:S(2)}, u32[]{:S(2)}) collective-permute-start(f32[72,1024]{1,0:T(8,128)S(1)} %get-tuple-element.32), channel_id=1, source_target_pairs={{0,32},{32,64},{64,96},{96,128},{128,160},{160,192},{192,224},{224... | collective-permute-start | bytes 884744 | tf_op jit(solution)/shard_map/ppermute | solution.py:558
  4.6 17.3 %collective-permute-start.1 = (f32[72,1024]{1,0:T(8,128)S(1)}, f32[72,1024]{1,0:T(8,128)S(1)}, u32[]{:S(2)}, u32[]{:S(2)}) collective-permute-start(f32[72,1024]{1,0:T(8,128)S(1)} %get-tuple-element.33), channel_id=1, source_target_pairs={{32,0},{64,32},{96,64},{128,96},{160,128},{192,160},{224,192},{256... | collective-permute-start | bytes 884744 | tf_op jit(solution)/shard_map/ppermute | solution.py:558
  5.9 16.0 %collective-permute-start.2 = (f32[24,1024]{1,0:T(8,128)S(1)}, f32[24,1024]{1,0:T(8,128)S(1)}, u32[]{:S(2)}, u32[]{:S(2)}) collective-permute-start(f32[24,1024]{1,0:T(8,128)S(1)} %get-tuple-element.34), channel_id=1, source_target_pairs={{0,1},{1,2},{2,3},{3,4},{4,5},{5,6},{6,7},{7,8},{8,9},{9,10},{10,1... | collective-permute-start | bytes 294920 | tf_op jit(solution)/shard_map/ppermute | solution.py:558
  12.0 9.9 %collective-permute-start.3 = (f32[24,1024]{1,0:T(8,128)S(1)}, f32[24,1024]{1,0:T(8,128)S(1)}, u32[]{:S(2)}, u32[]{:S(2)}) collective-permute-start(f32[24,1024]{1,0:T(8,128)S(1)} %get-tuple-element.35), channel_id=1, source_target_pairs={{1,0},{2,1},{3,2},{4,3},{5,4},{6,5},{7,6},{8,7},{9,8},{10,9},{11,1... | collective-permute-start | bytes 294920 | tf_op jit(solution)/shard_map/ppermute | solution.py:558
  23.5 17.4 %all-to-all-start = ((f32[8,2,32,128]{3,2,1,0:T(8,128)}), f32[8,2,32,128]{3,2,1,0:T(8,128)S(1)}, u32[]{:S(2)}, u32[]{:S(2)}) async-start(f32[8,2,32,128]{3,2,1,0:T(8,128)} %shard_map.102), calls=%async_computation | async-start | bytes 524288 | tf_op jit(solution)/shard_map/all_to_all | solution.py:580
  41.9 16.8 %all-to-all-start.1 = ((f32[8,2,32,128]{3,2,1,0:T(8,128)}), f32[8,2,32,128]{3,2,1,0:T(8,128)S(1)}, u32[]{:S(2)}, u32[]{:S(2)}) async-start(f32[8,2,32,128]{3,2,1,0:T(8,128)} %shard_map.103), calls=%async_computation.1 | async-start | bytes 524288 | tf_op jit(solution)/shard_map/all_to_all | solution.py:580
  58.8 2.8 %collective-permute-start.4 = (f32[80,1024]{1,0:T(8,128)S(1)}, f32[80,1024]{1,0:T(8,128)S(1)}, u32[]{:S(2)}, u32[]{:S(2)}) collective-permute-start(f32[80,1024]{1,0:T(8,128)S(1)} %shard_map.105.refs_0_.refs_1_), channel_id=1, source_target_pairs={{0,32},{32,64},{64,96},{96,128},{128,160},{160,192},{192,224},{224... | collective-permute-start | bytes 983048 | tf_op jit(solution)/shard_map/ppermute | solution.py:558
  60.2 5.8 %collective-permute-start.5 = (f32[80,1024]{1,0:T(8,128)S(1)}, f32[80,1024]{1,0:T(8,128)S(1)}, u32[]{:S(2)}, u32[]{:S(2)}) collective-permute-start(f32[80,1024]{1,0:T(8,128)S(1)} %shard_map.105.refs_0_.refs_1_), channel_id=1, source_target_pairs={{32,0},{64,32},{96,64},{128,96},{160,128},{192,160},{224,192},{256... | collective-permute-start | bytes 983048 | tf_op jit(solution)/shard_map/ppermute | solution.py:558
  66.6 9.5 %collective-permute-start.6 = (f32[24,1024]{1,0:T(8,128)S(1)}, f32[24,1024]{1,0:T(8,128)S(1)}, u32[]{:S(2)}, u32[]{:S(2)}) collective-permute-start(f32[24,1024]{1,0:T(8,128)S(1)} %get-tuple-element.38), channel_id=1, source_target_pairs={{0,1},{1,2},{2,3},{3,4},{4,5},{5,6},{6,7},{7,8},{8,9},{9,10},{10,1... | collective-permute-start | bytes 294920 | tf_op jit(solution)/shard_map/ppermute | solution.py:558
  68.7 9.0 %collective-permute-start.7 = (f32[24,1024]{1,0:T(8,128)S(1)}, f32[24,1024]{1,0:T(8,128)S(1)}, u32[]{:S(2)}, u32[]{:S(2)}) collective-permute-start(f32[24,1024]{1,0:T(8,128)S(1)} %get-tuple-element.39), channel_id=1, source_target_pairs={{1,0},{2,1},{3,2},{4,3},{5,4},{6,5},{7,6},{8,7},{9,8},{10,9},{11,1... | collective-permute-start | bytes 294920 | tf_op jit(solution)/shard_map/ppermute | solution.py:558
  79.6 39.9 %copy-start.15 = (f32[4,48,1024]{2,1,0:T(8,128)}, f32[4,48,1024]{2,1,0:T(8,128)S(1)}, u32[]{:S(2)}) copy-start(f32[4,48,1024]{2,1,0:T(8,128)S(1)} %get-tuple-element.48.refs_7_) | copy-start | bytes 2359300
  79.6 39.9 %copy-start.25 = (f32[8,1024]{1,0:T(8,128)}, f32[8,1024]{1,0:T(8,128)S(1)}, u32[]{:S(2)}) copy-start(f32[8,1024]{1,0:T(8,128)S(1)} %get-tuple-element.50.refs_9_) | copy-start | bytes 98308
  79.6 39.9 %copy-start.27 = (f32[48,128]{1,0:T(8,128)}, f32[48,128]{1,0:T(8,128)S(1)}, u32[]{:S(2)}) copy-start(f32[48,128]{1,0:T(8,128)S(1)} %get-tuple-element.49.refs_8_) | copy-start | bytes 73732
  79.6 39.9 %copy-start.11 = (f32[24,512]{1,0:T(8,128)}, f32[24,512]{1,0:T(8,128)S(1)}, u32[]{:S(2)}) copy-start(f32[24,512]{1,0:T(8,128)S(1)} %get-tuple-element.43.refs_3_.refs_1_.refs_4_) | copy-start | bytes 147460
  79.6 9.7 %collective-permute-start.8 = (f32[24,512]{1,0:T(8,128)S(1)}, f32[24,512]{1,0:T(8,128)S(1)}, u32[]{:S(2)}, u32[]{:S(2)}) collective-permute-start(f32[24,512]{1,0:T(8,128)S(1)} %get-tuple-element.42.refs_0_.refs_2_), channel_id=1, source_target_pairs={{0,32},{32,64},{64,96},{96,128},{128,160},{160,192},{192,224},{224... | collective-permute-start | bytes 147464 | tf_op jit(solution)/shard_map/ppermute | solution.py:558
  88.1 3.1 %collective-permute-start.9 = (f32[24,512]{1,0:T(8,128)S(1)}, f32[24,512]{1,0:T(8,128)S(1)}, u32[]{:S(2)}, u32[]{:S(2)}) collective-permute-start(f32[24,512]{1,0:T(8,128)S(1)} %get-tuple-element.42.refs_0_.refs_2_), channel_id=1, source_target_pairs={{32,0},{64,32},{96,64},{128,96},{160,128},{192,160},{224,192},{256... | collective-permute-start | bytes 147464 | tf_op jit(solution)/shard_map/ppermute | solution.py:558
  120.8 31.1 %all-to-all-start.3 = ((f32[512,1,128]{2,1,0:T(1,128)}), f32[512,1,128]{2,1,0:T(1,128)S(1)}, u32[]{:S(2)}, u32[]{:S(2)}) async-start(f32[512,1,128]{2,1,0:T(1,128)} %bitcast.6), calls=%async_computation.3 | async-start | bytes 524288 | tf_op jit(solution)/shard_map/all_to_all | solution.py:565
  135.1 0.7 collective-permute-start.10
  135.8 3.3 %collective-permute-start.11 = (f32[24,512]{1,0:T(8,128)S(1)}, f32[24,512]{1,0:T(8,128)S(1)}, u32[]{:S(2)}, u32[]{:S(2)}) collective-permute-start(f32[24,512]{1,0:T(8,128)S(1)} %shard_map.111.refs_1_), channel_id=1, source_target_pairs={{0,32},{32,64},{64,96},{96,128},{128,160},{160,192},{192,224},{224... | collective-permute-start | bytes 147464 | tf_op jit(solution)/shard_map/ppermute | solution.py:558
  137.9 4.5 %collective-permute-start.12 = (f32[24,512]{1,0:T(8,128)S(1)}, f32[24,512]{1,0:T(8,128)S(1)}, u32[]{:S(2)}, u32[]{:S(2)}) collective-permute-start(f32[24,512]{1,0:T(8,128)S(1)} %shard_map.111.refs_1_), channel_id=1, source_target_pairs={{32,0},{64,32},{96,64},{128,96},{160,128},{192,160},{224,192},{256... | collective-permute-start | bytes 147464 | tf_op jit(solution)/shard_map/ppermute | solution.py:558
  153.2 2.6 %collective-permute-start.13 = (f32[24,512]{1,0:T(8,128)S(1)}, f32[24,512]{1,0:T(8,128)S(1)}, u32[]{:S(2)}, u32[]{:S(2)}) collective-permute-start(f32[24,512]{1,0:T(8,128)S(1)} %shard_map.112.refs_0_), channel_id=1, source_target_pairs={{0,32},{32,64},{64,96},{96,128},{128,160},{160,192},{192,224},{224... | collective-permute-start | bytes 147464 | tf_op jit(solution)/shard_map/ppermute | solution.py:558
  154.5 4.5 %collective-permute-start.14 = (f32[24,512]{1,0:T(8,128)S(1)}, f32[24,512]{1,0:T(8,128)S(1)}, u32[]{:S(2)}, u32[]{:S(2)}) collective-permute-start(f32[24,512]{1,0:T(8,128)S(1)} %shard_map.112.refs_0_), channel_id=1, source_target_pairs={{32,0},{64,32},{96,64},{128,96},{160,128},{192,160},{224,192},{256... | collective-permute-start | bytes 147464 | tf_op jit(solution)/shard_map/ppermute | solution.py:558
  159.8 12.0 %all-to-all-start.4 = ((f32[4,16,512]{2,1,0:T(8,128)}), f32[4,16,512]{2,1,0:T(8,128)S(1)}, u32[]{:S(2)}, u32[]{:S(2)}) async-start(f32[4,16,512]{2,1,0:T(8,128)} %shard_map.113), calls=%async_computation.4 | async-start | bytes 262144 | tf_op jit(solution)/shard_map/all_to_all | solution.py:571
  163.1 51.4 %copy-start.2 = (f32[4,256,256]{2,1,0:T(8,128)S(1)}, f32[4,256,256]{2,1,0:T(8,128)}, u32[]{:S(2)}) copy-start(f32[4,256,256]{2,1,0:T(8,128)} %refs_11_.1) | copy-start | bytes 3145732
  163.1 51.4 %copy-start.24 = (f32[1024]{0:T(1024)S(1)}, f32[1024]{0:T(1024)}, u32[]{:S(2)}) copy-start(f32[1024]{0:T(1024)} %param.14) | copy-start | bytes 12292
  163.1 51.4 %copy-start.26 = (f32[8,1024]{1,0:T(8,128)S(1)}, f32[8,1024]{1,0:T(8,128)}, u32[]{:S(2)}) copy-start(f32[8,1024]{1,0:T(8,128)} %copy-done.25) | copy-start | bytes 98308
  163.1 51.4 %copy-start.28 = (f32[48,128]{1,0:T(8,128)S(1)}, f32[48,128]{1,0:T(8,128)}, u32[]{:S(2)}) copy-start(f32[48,128]{1,0:T(8,128)} %copy-done.27) | copy-start | bytes 73732
  163.3 51.2 %copy-start.14 = (f32[4,48,1024]{2,1,0:T(8,128)S(1)}, f32[4,48,1024]{2,1,0:T(8,128)}, u32[]{:S(2)}) copy-start(f32[4,48,1024]{2,1,0:T(8,128)} %copy-done.13) | copy-start | bytes 2359300
  197.2 12.9 %collective-permute-start.15 = (f32[24,512]{1,0:T(8,128)S(1)}, f32[24,512]{1,0:T(8,128)S(1)}, u32[]{:S(2)}, u32[]{:S(2)}) collective-permute-start(f32[24,512]{1,0:T(8,128)S(1)} %shard_map.116.refs_0_), channel_id=1, source_target_pairs={{0,32},{32,64},{64,96},{96,128},{128,160},{160,192},{192,224},{224... | collective-permute-start | bytes 147464 | tf_op jit(solution)/shard_map/ppermute | solution.py:558
  199.7 10.3 %collective-permute-start.16 = (f32[24,512]{1,0:T(8,128)S(1)}, f32[24,512]{1,0:T(8,128)S(1)}, u32[]{:S(2)}, u32[]{:S(2)}) collective-permute-start(f32[24,512]{1,0:T(8,128)S(1)} %shard_map.116.refs_0_), channel_id=1, source_target_pairs={{32,0},{64,32},{96,64},{128,96},{160,128},{192,160},{224,192},{256... | collective-permute-start | bytes 147464 | tf_op jit(solution)/shard_map/ppermute | solution.py:558
  201.0 9.3 %collective-permute-start.17 = (f32[24,512]{1,0:T(8,128)S(1)}, f32[24,512]{1,0:T(8,128)S(1)}, u32[]{:S(2)}, u32[]{:S(2)}) collective-permute-start(f32[24,512]{1,0:T(8,128)S(1)} %shard_map.116.refs_0_), channel_id=1, source_target_pairs={{0,64},{32,96},{64,128},{96,160},{128,192},{160,224},{192,256},{22... | collective-permute-start | bytes 147464 | tf_op jit(solution)/shard_map/ppermute | solution.py:558
  208.5 6.0 %collective-permute-start.18 = (f32[24,512]{1,0:T(8,128)S(1)}, f32[24,512]{1,0:T(8,128)S(1)}, u32[]{:S(2)}, u32[]{:S(2)}) collective-permute-start(f32[24,512]{1,0:T(8,128)S(1)} %shard_map.116.refs_0_), channel_id=1, source_target_pairs={{64,0},{96,32},{128,64},{160,96},{192,128},{224,160},{256,192},{28... | collective-permute-start | bytes 147464 | tf_op jit(solution)/shard_map/ppermute | solution.py:558
  (25 other events, 400.9 us)
